TPU v7x, 32 devices: a whole 2x2x4 slice. The times are simulated.
32 devices in a mesh: parts: 2 (over y), seq: 4 (over z), chan: 2 (over x), rep: 2 (over core).
Axes of the slice: x: 2, y: 2, z: 4, core: 2. Of those that a mesh axis runs over, the one named last changes fastest.
Arguments:
- tokens: bfloat16 [4096, 4096], P(('parts', 'seq'), ('chan', 'rep')), parts along dimension 0, may hold values from -6 to 6
- w_query: bfloat16 [4096, 4096], P('seq', ('chan', 'rep')), may hold values from -0.09375 to 0.09375
- w_key: bfloat16 [4096, 4096], P('seq', ('chan', 'rep')), may hold values from -0.09375 to 0.09375
- w_value: bfloat16 [4096, 4096], P('seq', ('chan', 'rep')), may hold values from -0.09375 to 0.09375
- decay_rate: float32 [4096, 16], P(('chan', 'rep', 'seq')), may hold values from 4.8828125e-06 to 0.04, as said below
- residue: float32 [4096, 16], P(('chan', 'rep', 'seq')), may hold values from -1.5 to 1.5
- carried: float32 [8192, 16], P(('parts', 'chan', 'rep', 'seq')), parts along dimension 0, may hold values from -6 to 6
Outputs:
- gated_output: bfloat16 [4096, 4096], P(('parts', 'seq'), ('chan', 'rep')), parts along dimension 0
- new_state: float32 [8192, 16], P(('parts', 'chan', 'rep', 'seq')), parts along dimension 0
There are 2 independent parts, one for each index of `parts`. A program takes and returns all parts, laid end to end along the dimension named above; an argument that names none is the same for every part. Nothing has to cross between parts.
Inputs may be any that keep to these rules, and one draw needn't show every extreme that they name: `decay_rate`: each rate lies between 0.01 / 2048 and 0.04.
All inputs are finite; a program needn't handle non-finite values.
Results may differ from a plain program's by a relative error of at most 0.0066.
Values may be sent and summed in bfloat16 or wider, within the bound.
A program may use at most 128 MiB of HBM per device.

v0:
```python
import functools

import jax
import jax.numpy as jnp
from jax import lax
from jax.experimental import pallas as pl
from jax.experimental.pallas import tpu as pltpu
from jax.sharding import PartitionSpec as P

BLOCK = 128
LANES = 128
CHUNKS = 8
MESH = pl.DeviceIdType.MESH


HIGHEST_PRECISION = lax.Precision.HIGHEST


def mode_scale(decay_rates):
    return jnp.sqrt(-jnp.expm1(-2.0 * decay_rates))


def local_ends(blocks, decay_rates):
    block_width = blocks.shape[2]
    offsets = jnp.arange(block_width, dtype=jnp.float32)
    tail_powers = jnp.exp(-decay_rates[:, :, None] * (block_width - 1.0 - offsets)[None, None, :])
    sums_here = jnp.einsum("cnb,cmb->cnm", blocks, tail_powers, precision=HIGHEST_PRECISION)
    return mode_scale(decay_rates)[:, None, :] * sums_here


def combine_states(earlier, later):
    return (earlier[0] * later[0], later[0] * earlier[1] + later[1])


def block_sums(block_ends, decay_rates, block_width):
    step_decay = jnp.broadcast_to(jnp.exp(-decay_rates * block_width)[:, None, :], block_ends.shape)
    unused_decay, running = lax.associative_scan(combine_states, (step_decay, block_ends), axis=1)
    return running


def entering_states(running, decay_rates, start_state, block_width):
    count_blocks = running.shape[1]
    block_starts = jnp.arange(count_blocks, dtype=jnp.float32) * block_width
    decayed = (
        jnp.exp(-decay_rates[:, None, :] * block_starts[None, :, None]) * start_state[:, None, :]
    )
    earlier_sums = jnp.concatenate([jnp.zeros_like(running[:, :1]), running[:, :-1]], axis=1)
    final_state = (
        jnp.exp(-decay_rates * (count_blocks * block_width)) * start_state + running[:, -1]
    )
    return (decayed + earlier_sums, final_state)


def block_convolve(blocks, decay_rates, residues, entering):
    block_width = blocks.shape[2]
    offsets = jnp.arange(block_width, dtype=jnp.float32)
    powers = jnp.exp(-decay_rates[:, :, None] * offsets[None, None, :])
    kernel = jnp.sum((residues * mode_scale(decay_rates))[:, :, None] * powers, axis=1)
    out_index = jnp.arange(block_width, dtype=jnp.int32)[:, None]
    in_index = jnp.arange(block_width, dtype=jnp.int32)[None, :]
    lag = jnp.maximum(out_index - in_index, 0)
    causal = (out_index >= in_index).astype(jnp.float32)
    toeplitz = kernel[:, lag] * causal[None, :, :]
    direct = jnp.einsum("cij,cnj->cni", toeplitz, blocks, precision=HIGHEST_PRECISION)
    leading = residues[:, :, None] * jnp.exp(
        -decay_rates[:, :, None] * (offsets + 1.0)[None, None, :]
    )
    return direct + jnp.einsum("cnm,cmb->cnb", entering, leading, precision=HIGHEST_PRECISION)


def per_device(tokens, w_query, w_key, w_value, decay_rate, residue, carried):
    gathered = lax.all_gather(tokens, ("chan", "rep"), axis=1, tiled=True)
    pieces = (
        lax.all_gather(w_query, "seq", axis=0, tiled=True),
        lax.all_gather(w_key, "seq", axis=0, tiled=True),
        lax.all_gather(w_value, "seq", axis=0, tiled=True),
    )
    query_acc, key_acc, value_acc = tuple(
        (
            lax.dot_general(
                weight_piece, gathered, (((0,), (1,)), ((), ())), preferred_element_type=jnp.float32
            )
            for weight_piece in pieces
        )
    )
    query_rows = query_acc.astype(jnp.bfloat16)
    key_rows = key_acc.astype(jnp.bfloat16)
    value_rows = value_acc.astype(jnp.bfloat16)
    query_rows, key_rows, value_rows = lax.optimization_barrier((query_rows, key_rows, value_rows))
    product = (key_rows.astype(jnp.float32) * value_rows.astype(jnp.float32)).astype(jnp.bfloat16)
    owned = lax.all_to_all(product, "seq", split_axis=0, concat_axis=1, tiled=True)
    own_chan = owned.shape[0]
    blocks = owned.astype(jnp.float32).reshape(own_chan, -1, BLOCK)
    block_end = local_ends(blocks, decay_rate)
    running = block_sums(block_end, decay_rate, BLOCK)
    entering, new_state = entering_states(running, decay_rate, carried, BLOCK)
    conv_out = (
        block_convolve(blocks, decay_rate, residue, entering)
        .reshape(own_chan, -1)
        .astype(jnp.bfloat16)
    )
    conv_back = lax.all_to_all(conv_out, "seq", split_axis=1, concat_axis=0, tiled=True)
    conv_back = lax.optimization_barrier(conv_back)
    gated_rows = (query_rows.astype(jnp.float32) * conv_back.astype(jnp.float32)).astype(
        jnp.bfloat16
    )
    return (gated_rows.T, new_state)


def scan_kernel(count, q_ref, k_ref, v_ref, rate_hbm, scale_hbm, residue_hbm, carried_hbm, out_ref,
                state_ref, rate_ref, scale_ref, residue_ref, carried_ref, signal, ends, entering, conv,
                gated_ref, fill_sem, own_sem, send_sem, recv_sem):
    seq = lax.axis_index("seq")
    barrier = pltpu.get_barrier_semaphore()
    for step in range(1, count):
        pl.semaphore_signal(
            barrier, inc=1, device_id={"seq": lax.rem(seq + step, count)}, device_id_type=MESH
        )
    fills = [
        pltpu.make_async_copy(source, target, fill_sem.at[n])
        for n, (source, target) in enumerate((
            (rate_hbm, rate_ref), (scale_hbm, scale_ref),
            (residue_hbm, residue_ref), (carried_hbm, carried_ref),
        ))
    ]
    for fill in fills:
        fill.start()
    length, width = q_ref.shape
    rows_out = length // count

    def columns_of(source, lane):
        return out_ref.at[:, pl.ds(pl.multiple_of(source * width + lane, LANES), LANES)]

    def block_of(target, lane):
        top = pl.multiple_of(target * rows_out, rows_out)
        return gated_ref.at[pl.ds(top, rows_out), pl.ds(lane, LANES)]

    def give(step, lane):
        target = lax.rem(seq + step, count)
        group = lane // LANES
        return pltpu.make_async_remote_copy(
            src_ref=block_of(target, lane), dst_ref=columns_of(seq, lane),
            send_sem=send_sem.at[target, group], recv_sem=recv_sem.at[seq, group],
            device_id={"seq": target}, device_id_type=MESH,
        )

    def take(step, lane):
        source = lax.rem(seq + step, count)
        group = lane // LANES
        return pltpu.make_async_remote_copy(
            src_ref=columns_of(source, lane), dst_ref=columns_of(source, lane),
            send_sem=send_sem.at[source, group], recv_sem=recv_sem.at[source, group],
            device_id={"seq": source}, device_id_type=MESH,
        )

    def keep(lane):
        return pltpu.make_async_copy(
            block_of(seq, lane), columns_of(seq, lane), own_sem.at[lane // LANES]
        )

    modes = rate_ref.shape[0]
    chunk = length // CHUNKS
    rows_at = 256
    for lane in range(0, width, LANES):
        lanes = pl.ds(lane, LANES)

        def multiply(step, _):
            rows = pl.ds(pl.multiple_of(step * rows_at, rows_at), rows_at)
            product = k_ref[rows, lanes].astype(jnp.float32) * v_ref[rows, lanes].astype(jnp.float32)
            signal[rows, :] = product.astype(jnp.bfloat16).astype(jnp.float32)
            return 0

        lax.fori_loop(0, length // rows_at, multiply, 0)
        if lane == 0:
            for fill in fills:
                fill.wait()
        rates = rate_ref[:, lanes]
        residues = residue_ref[:, lanes]
        scale = scale_ref[:, lanes]
        decay = jnp.exp(-rates)
        weight = residues * scale
        chunk_decay = jnp.exp(-rates * chunk)

        def rows_of(array):
            return [jnp.broadcast_to(array[m : m + 1, :], (CHUNKS, LANES)) for m in range(modes)]

        decays = rows_of(decay)
        weights = rows_of(weight)

        def sums(step, states):
            here = signal[pl.ds(step, CHUNKS, stride=chunk), :]
            return tuple(d * s + here for d, s in zip(decays, states))

        zero = jnp.zeros((CHUNKS, LANES), jnp.float32)
        finals = lax.fori_loop(0, chunk, sums, (zero,) * modes, unroll=4)
        for m in range(modes):
            ends[m] = finals[m]
        state = carried_ref[:, lanes]
        for c in range(CHUNKS):
            entering[:, c, :] = residues * state
            state = chunk_decay * state + scale * ends[:, c, :]
        state_ref[:, lanes] = state

        def outputs(step, states):
            here = signal[pl.ds(step, CHUNKS, stride=chunk), :]
            states = tuple(d * s + w * here for d, s, w in zip(decays, states, weights))
            terms = list(states)
            while len(terms) > 1:
                terms = [a + b for a, b in zip(terms[::2], terms[1::2])] + (
                    [terms[-1]] if len(terms) % 2 else []
                )
            conv[pl.ds(step, CHUNKS, stride=chunk), :] = terms[0]
            return states

        starts = tuple(entering[m] for m in range(modes))
        lax.fori_loop(0, chunk, outputs, starts, unroll=4)

        def gate(step, _):
            rows = pl.ds(pl.multiple_of(step * rows_at, rows_at), rows_at)
            rounded = conv[rows, :].astype(jnp.bfloat16).astype(jnp.float32)
            gated_ref[rows, lanes] = (q_ref[rows, lanes].astype(jnp.float32) * rounded).astype(
                jnp.bfloat16
            )
            return 0

        lax.fori_loop(0, length // rows_at, gate, 0)
        if lane == 0:
            pl.semaphore_wait(barrier, count - 1)
        for step in range(1, count):
            give(step, lane).start()
        keep(lane).start()
    for lane in range(0, width, LANES):
        keep(lane).wait()
        for step in range(1, count):
            take(step, lane).wait_recv()
            give(step, lane).wait_send()


def gated_scan(rows, rate, residue, carried, count):
    length = rows.shape[1]
    width, modes = rate.shape
    vmem = pl.BlockSpec(memory_space=pltpu.VMEM)
    anywhere = pl.BlockSpec(memory_space=pl.ANY)
    dma = pltpu.SemaphoreType.DMA
    table = pltpu.VMEM((modes, width), jnp.float32)
    gated, state = pl.pallas_call(
        functools.partial(scan_kernel, count),
        grid=(1,),
        out_shape=(
            jax.ShapeDtypeStruct((length // count, width * count), jnp.bfloat16),
            jax.ShapeDtypeStruct((modes, width), jnp.float32),
        ),
        in_specs=[pl.BlockSpec((None, length, width), functools.partial(lambda j, i: (j, 0, 0), j)) for j in range(3)]
        + [anywhere] * 4,
        out_specs=(anywhere, vmem),
        scratch_shapes=[table] * 4 + [
            pltpu.VMEM((length, LANES), jnp.float32),
            pltpu.VMEM((modes, CHUNKS, LANES), jnp.float32),
            pltpu.VMEM((modes, CHUNKS, LANES), jnp.float32),
            pltpu.VMEM((length, LANES), jnp.float32),
            pltpu.VMEM((length, width), jnp.bfloat16),
            dma((4,)), dma((width // LANES,)),
            dma((count, width // LANES)), dma((count, width // LANES)),
        ],
        compiler_params=pltpu.CompilerParams(
            collective_id=1, has_side_effects=True, vmem_limit_bytes=60 * 2**20
        ),
    )(rows, rows, rows, rate.T, mode_scale(rate).T, residue.T, carried.T)
    return gated, state.T


PIECES = 4


def project_kernel(count, tokens_ref, query_ref, key_ref, value_ref, out_ref,
                   all_ref, weights_ref, fill_sem,
                  hop_send, hop_recv, side_send, side_recv, core_send, core_recv,
                  part_send, part_recv, layer_send, layer_recv):
    part, seq, chan, rep = (lax.axis_index(a) for a in ("parts", "seq", "chan", "rep"))
    rows, columns = tokens_ref.shape
    depth, outer = query_ref.shape
    width = outer // count
    half = depth // 2
    piece = rows // PIECES
    own_columns = pl.ds(pl.multiple_of(seq * width, width), width)
    matrices = (query_ref, key_ref, value_ref)

    barrier = pltpu.get_barrier_semaphore()
    mates = ({"parts": 1 - part}, {"chan": 1 - chan}, {"rep": 1 - rep})
    for mate in mates:
        pl.semaphore_signal(barrier, inc=1, device_id=mate, device_id_type=MESH)
    for step in range(1, count):
        pl.semaphore_signal(
            barrier, inc=1, device_id={"seq": lax.rem(seq + step, count)}, device_id_type=MESH
        )
    pl.semaphore_wait(barrier, count - 1 + len(mates))

    def token_block(block, side, core, p):
        top = pl.multiple_of(block * rows + p * piece, piece)
        left = pl.multiple_of((side * 2 + core) * columns, columns)
        return all_ref.at[pl.ds(top, piece), pl.ds(left, columns)]

    def own_piece(p):
        return tokens_ref.at[pl.ds(p * piece, piece), :]

    def remote(source, target, send, recv, device):
        return pltpu.make_async_remote_copy(
            src_ref=source, dst_ref=target, send_sem=send, recv_sem=recv,
            device_id=device, device_id_type=MESH,
        )

    def hop(block, p, way, source=None):
        here = token_block(block, chan, rep, p)
        device = {"seq": seq + way}
        return remote(here if source is None else source, here, hop_send.at[block, p, (1 - way) // 2], hop_recv.at[block, p], device)

    def side(block, p, source=None):
        here = token_block(block, chan, rep, p)
        return remote(here if source is None else source, here, side_send.at[block, p], side_recv.at[block, p], {"chan": 1 - chan})

    def side_arrival(block, p):
        there = token_block(block, 1 - chan, rep, p)
        return remote(there, there, side_send.at[block, p], side_recv.at[block, p], {"chan": 1 - chan})

    def core(block, which, p, source=None):
        here = token_block(block, chan if which == 0 else 1 - chan, rep, p)
        return remote(here if source is None else source, here, core_send.at[block, which, p], core_recv.at[block, which, p], {"rep": 1 - rep})

    def core_arrival(block, which, p):
        there = token_block(block, chan if which == 0 else 1 - chan, 1 - rep, p)
        return remote(there, there, core_send.at[block, which, p], core_recv.at[block, which, p], {"rep": 1 - rep})

    def weight_block(block, m, part_of):
        top = pl.multiple_of(block * depth + part_of * half, half)
        return weights_ref.at[m, pl.ds(top, half), :]

    def spread(target, m):
        source = matrices[m].at[
            pl.ds(pl.multiple_of(part * half, half), half),
            pl.ds(pl.multiple_of(target * width, width), width),
        ]
        return remote(source, weight_block(seq, m, part), layer_send.at[target, m], layer_recv.at[seq, m], {"seq": target})

    def spread_arrival(block, m):
        here = weight_block(block, m, part)
        return remote(here, here, layer_send.at[block, m], layer_recv.at[block, m], {"seq": block})

    def swap(block, m):
        here = weight_block(block, m, part)
        return remote(here, here, part_send.at[block, m], part_recv.at[block, m], {"parts": 1 - part})

    def swap_arrival(block, m):
        there = weight_block(block, m, 1 - part)
        return remote(there, there, part_send.at[block, m], part_recv.at[block, m], {"parts": 1 - part})

    inward = 1 - 2 * ((2 * seq) // count)

    def inside(other):
        return (other >= 0) & (other < count)

    def sources(distance):
        near, far = seq - inward * distance, seq + inward * distance
        return ((inside(near), near, inward), (inside(far), far, -inward))

    def has_next(way):
        return inside(seq + way)

    def send_weights(distance):
        for there, other, _ in sources(distance):
            @pl.when(there)
            def _():
                for m in range(3):
                    spread(other, m).start()

    def project(block):
        top = pl.multiple_of(block * rows, rows)

        def one(m, _):
            out_ref[m, pl.ds(top, rows), :] = jnp.dot(
                all_ref[pl.ds(top, rows), :], weights_ref[m], preferred_element_type=jnp.float32
            ).astype(jnp.bfloat16)
            return 0

        lax.fori_loop(0, 3, one, 0)

    fills = [
        pltpu.make_async_copy(
            tokens_ref,
            all_ref.at[pl.ds(pl.multiple_of(seq * rows, rows), rows),
                       pl.ds(pl.multiple_of((chan * 2 + rep) * columns, columns), columns)],
            fill_sem.at[3])
    ] + [
        pltpu.make_async_copy(
            matrices[m].at[:, own_columns],
            weights_ref.at[m, pl.ds(pl.multiple_of(seq * depth, depth), depth), :],
            fill_sem.at[m])
        for m in range(3)
    ]
    for distance in range(1, count):
        send_weights(distance)
    for p in range(PIECES):
        for way in (1, -1):
            @pl.when(has_next(way))
            def _():
                hop(seq, p, way, own_piece(p)).start()
        side(seq, p, own_piece(p)).start()
        core(seq, 0, p, own_piece(p)).start()
    for fill in fills:
        fill.start()

    def pass_side(block):
        for p in range(PIECES):
            side_arrival(block, p).wait_recv()
            core(block, 1, p).start()

    pass_side(seq)
    for distance in range(1, count):
        for m in range(3):
            for there, other, _ in sources(distance):
                @pl.when(there)
                def _():
                    spread_arrival(other, m).wait_recv()
                    swap(other, m).start()
    for fill in fills:
        fill.wait()

    def core_arrivals(block):
        for p in range(PIECES):
            for which in range(2):
                core_arrival(block, which, p).wait_recv()

    def finish(distance):
        if distance == 0:
            core_arrivals(seq)
            project(seq)
        else:
            for there, other, _ in sources(distance):
                @pl.when(there)
                def _():
                    pass_side(other)
                    core_arrivals(other)
                    project(other)

    for distance in range(1, count):
        for there, other, way in sources(distance):
            for p in range(PIECES):
                @pl.when(there)
                def _():
                    hop(other, p, way).wait_recv()

                    @pl.when(has_next(way))
                    def _():
                        hop(other, p, way).start()

                    side(other, p).start()
                    core(other, 0, p).start()
        if distance == 1:
            for there, other, _ in [s for d in range(1, count) for s in sources(d)]:
                @pl.when(there)
                def _():
                    for m in range(3):
                        swap_arrival(other, m).wait_recv()
        finish(distance - 1)
    finish(count - 1)

    for p in range(PIECES):
        for way in (1, -1):
            @pl.when(has_next(way))
            def _():
                hop(seq, p, way, own_piece(p)).wait_send()
        side(seq, p, own_piece(p)).wait_send()
        core(seq, 0, p, own_piece(p)).wait_send()
        core(seq, 1, p).wait_send()
    for distance in range(1, count):
        for there, other, way in sources(distance):
            @pl.when(there)
            def _():
                for p in range(PIECES):
                    @pl.when(has_next(way))
                    def _():
                        hop(other, p, way).wait_send()

                    side(other, p).wait_send()
                    for which in range(2):
                        core(other, which, p).wait_send()
                for m in range(3):
                    spread(other, m).wait_send()
                    swap(other, m).wait_send()


def project_all(tokens, w_query, w_key, w_value, count):
    rows, columns = tokens.shape
    depth, outer = w_query.shape
    width = outer // count
    anywhere = pl.BlockSpec(memory_space=pl.ANY)
    dma = pltpu.SemaphoreType.DMA
    return pl.pallas_call(
        functools.partial(project_kernel, count),
        out_shape=jax.ShapeDtypeStruct((3, rows * count, width), jnp.bfloat16),
        in_specs=[anywhere] * 4,
        out_specs=pl.BlockSpec(memory_space=pltpu.VMEM),
        scratch_shapes=[
            pltpu.VMEM((rows * count, columns * 4), jnp.bfloat16),
            pltpu.VMEM((3, depth * count, width), jnp.bfloat16),
            dma((4,)),
            dma((count, PIECES, 2)), dma((count, PIECES)),
            dma((count, PIECES)), dma((count, PIECES)),
            dma((count, 2, PIECES)), dma((count, 2, PIECES)),
            dma((count, 3)), dma((count, 3)),
            dma((count, 3)), dma((count, 3)),
        ],
        compiler_params=pltpu.CompilerParams(
            collective_id=0, has_side_effects=True, vmem_limit_bytes=63 * 2**20
        ),
    )(tokens, w_query, w_key, w_value)


def per_device_channels(tokens, w_query, w_key, w_value, decay_rate, residue, carried):
    count = lax.axis_size("seq")
    rows = project_all(tokens, w_query, w_key, w_value, count)
    return gated_scan(rows, decay_rate, residue, carried, count)


def solution(mesh):
    in_specs = (
        P(("parts", "seq"), ("chan", "rep")),
        P("seq", ("chan", "rep")),
        P("seq", ("chan", "rep")),
        P("seq", ("chan", "rep")),
        P(("chan", "rep", "seq"), None),
        P(("chan", "rep", "seq"), None),
        P(("parts", "chan", "rep", "seq"), None),
    )
    out_specs = (P(("parts", "seq"), ("chan", "rep")), P(("parts", "chan", "rep", "seq"), None))

    def body(*arrays):
        own_channels = arrays[4].shape[0]
        mates = all(mesh.shape[a] == 2 for a in ("parts", "chan", "rep"))
        chosen = per_device_channels if own_channels % LANES == 0 and mates else per_device
        return chosen(*arrays)

    return jax.shard_map(body, mesh=mesh, in_specs=in_specs, out_specs=out_specs, check_vma=False)
```

profile of v0, /device:TPU:25, one launch (start us, length us, event | category | flops | bytes accessed | tf_op | source)
XLA Modules:
  0.0 185.3 jit_solution(18199856473558594193)
XLA Ops:
  0.6 1.3 sqrt_bitcast_fusion.scale_hbm
  2.0 152.4 %shard_map.86.q_ref.k_ref.v_ref = bf16[3,2048,256]{2,1,0:T(8,128)(2,1)} custom-call(bf16[512,1024]{1,0:T(8,128)(2,1)} %tokens_ref.1, bf16[1024,1024]{1,0:T(8,128)(2,1)} %query_ref.1, bf16[1024,1024]{1,0:T(8,128)(2,1)} %key_ref.1, bf16[1024,1024]{1,0:T(8,128)(2,1)} %value_ref.1), custom_call_target="tpu_custom_call" | custom-call | tf_op jit(solution)/shard_map/pallas_call | solution.py:497
  154.3 28.0 %shard_map.87 = (bf16[512,1024]{1,0:T(8,128)(2,1)}, f32[16,256]{1,0:T(8,128)}) custom-call(bf16[3,2048,256]{2,1,0:T(8,128)(2,1)} %shard_map.86.q_ref.k_ref.v_ref, bf16[3,2048,256]{2,1,0:T(8,128)(2,1)} %shard_map.86.q_ref.k_ref.v_ref, bf16[3,2048,256]{2,1,0:T(8,128)(2,1)} %shard_map.86.q_ref.k_ref.v_ref, f32[16,256]{1,0:T(8,128)} %bitcast.6, ...), custom_call_target="tpu_custom_call" | custom-call | tf_op jit(solution)/shard_map/pallas_call | solution.py:246
  182.4 0.0 copy-start
  182.4 2.3 %copy.11 = bf16[512,1024]{1,0:T(8,128)(2,1)} copy(bf16[512,1024]{1,0:T(8,128)(2,1)} %get-tuple-element.8) | data formatting | bytes 2097152
  184.7 0.0 copy-done
  184.7 0.6 copy.12
Async XLA Ops:
  182.4 2.3 %copy-start = (f32[16,256]{1,0:T(8,128)S(1)}, f32[16,256]{1,0:T(8,128)}, u32[]{:S(2)}) copy-start(f32[16,256]{1,0:T(8,128)} %get-tuple-element.5) | copy-start | bytes 49156
where the time goes:
time: 186 us; the launch traced here: 185 us
  Pallas kernels  180 us (97%)
  local copies, waits for them, and re-layouts  2.88 us (2%)
    pallas_call x1, Pallas kernels, project_all(): pl.pallas_call(functools.partial(project_kernel, count), out_shape=jax.Sh...  152 us
    pallas_call x1, Pallas kernels, gated_scan(): pl.pallas_call(functools.partial(scan_kernel, count), grid=(1,), out_shap...  28 us

commit v1 on v0

v1 whole, which is shorter than its diff:
```python
import functools

import jax
import jax.numpy as jnp
from jax import lax
from jax.experimental import pallas as pl
from jax.experimental.pallas import tpu as pltpu
from jax.sharding import PartitionSpec as P

BLOCK = 128
LANES = 128
CHUNKS = 8
MESH = pl.DeviceIdType.MESH


HIGHEST_PRECISION = lax.Precision.HIGHEST


def mode_scale(decay_rates):
    return jnp.sqrt(-jnp.expm1(-2.0 * decay_rates))


def local_ends(blocks, decay_rates):
    block_width = blocks.shape[2]
    offsets = jnp.arange(block_width, dtype=jnp.float32)
    tail_powers = jnp.exp(-decay_rates[:, :, None] * (block_width - 1.0 - offsets)[None, None, :])
    sums_here = jnp.einsum("cnb,cmb->cnm", blocks, tail_powers, precision=HIGHEST_PRECISION)
    return mode_scale(decay_rates)[:, None, :] * sums_here


def combine_states(earlier, later):
    return (earlier[0] * later[0], later[0] * earlier[1] + later[1])


def block_sums(block_ends, decay_rates, block_width):
    step_decay = jnp.broadcast_to(jnp.exp(-decay_rates * block_width)[:, None, :], block_ends.shape)
    unused_decay, running = lax.associative_scan(combine_states, (step_decay, block_ends), axis=1)
    return running


def entering_states(running, decay_rates, start_state, block_width):
    count_blocks = running.shape[1]
    block_starts = jnp.arange(count_blocks, dtype=jnp.float32) * block_width
    decayed = (
        jnp.exp(-decay_rates[:, None, :] * block_starts[None, :, None]) * start_state[:, None, :]
    )
    earlier_sums = jnp.concatenate([jnp.zeros_like(running[:, :1]), running[:, :-1]], axis=1)
    final_state = (
        jnp.exp(-decay_rates * (count_blocks * block_width)) * start_state + running[:, -1]
    )
    return (decayed + earlier_sums, final_state)


def block_convolve(blocks, decay_rates, residues, entering):
    block_width = blocks.shape[2]
    offsets = jnp.arange(block_width, dtype=jnp.float32)
    powers = jnp.exp(-decay_rates[:, :, None] * offsets[None, None, :])
    kernel = jnp.sum((residues * mode_scale(decay_rates))[:, :, None] * powers, axis=1)
    out_index = jnp.arange(block_width, dtype=jnp.int32)[:, None]
    in_index = jnp.arange(block_width, dtype=jnp.int32)[None, :]
    lag = jnp.maximum(out_index - in_index, 0)
    causal = (out_index >= in_index).astype(jnp.float32)
    toeplitz = kernel[:, lag] * causal[None, :, :]
    direct = jnp.einsum("cij,cnj->cni", toeplitz, blocks, precision=HIGHEST_PRECISION)
    leading = residues[:, :, None] * jnp.exp(
        -decay_rates[:, :, None] * (offsets + 1.0)[None, None, :]
    )
    return direct + jnp.einsum("cnm,cmb->cnb", entering, leading, precision=HIGHEST_PRECISION)


def per_device(tokens, w_query, w_key, w_value, decay_rate, residue, carried):
    gathered = lax.all_gather(tokens, ("chan", "rep"), axis=1, tiled=True)
    pieces = (
        lax.all_gather(w_query, "seq", axis=0, tiled=True),
        lax.all_gather(w_key, "seq", axis=0, tiled=True),
        lax.all_gather(w_value, "seq", axis=0, tiled=True),
    )
    query_acc, key_acc, value_acc = tuple(
        (
            lax.dot_general(
                weight_piece, gathered, (((0,), (1,)), ((), ())), preferred_element_type=jnp.float32
            )
            for weight_piece in pieces
        )
    )
    query_rows = query_acc.astype(jnp.bfloat16)
    key_rows = key_acc.astype(jnp.bfloat16)
    value_rows = value_acc.astype(jnp.bfloat16)
    query_rows, key_rows, value_rows = lax.optimization_barrier((query_rows, key_rows, value_rows))
    product = (key_rows.astype(jnp.float32) * value_rows.astype(jnp.float32)).astype(jnp.bfloat16)
    owned = lax.all_to_all(product, "seq", split_axis=0, concat_axis=1, tiled=True)
    own_chan = owned.shape[0]
    blocks = owned.astype(jnp.float32).reshape(own_chan, -1, BLOCK)
    block_end = local_ends(blocks, decay_rate)
    running = block_sums(block_end, decay_rate, BLOCK)
    entering, new_state = entering_states(running, decay_rate, carried, BLOCK)
    conv_out = (
        block_convolve(blocks, decay_rate, residue, entering)
        .reshape(own_chan, -1)
        .astype(jnp.bfloat16)
    )
    conv_back = lax.all_to_all(conv_out, "seq", split_axis=1, concat_axis=0, tiled=True)
    conv_back = lax.optimization_barrier(conv_back)
    gated_rows = (query_rows.astype(jnp.float32) * conv_back.astype(jnp.float32)).astype(
        jnp.bfloat16
    )
    return (gated_rows.T, new_state)


PIECES = 4
EARLY = 2


def layer_kernel(count, tokens_ref, query_ref, key_ref, value_ref, rate_hbm, scale_hbm, residue_hbm,
                 carried_hbm, out_ref, state_ref,
                 all_ref, weights_ref, query_rows, signal, conv, gated_ref, ends, entering,
                 rate_ref, scale_ref, residue_ref, carried_ref,
                 fill_sem, hop_send, hop_recv, side_send, side_recv, core_send, core_recv,
                 part_send, part_recv, layer_send, layer_recv, out_send, out_recv, own_sem):
    part, seq, chan, rep = (lax.axis_index(a) for a in ("parts", "seq", "chan", "rep"))
    rows, columns = tokens_ref.shape
    depth, outer = query_ref.shape
    width = outer // count
    half = depth // 2
    piece = rows // PIECES
    modes = rate_ref.shape[0]
    own_columns = pl.ds(pl.multiple_of(seq * width, width), width)
    matrices = (query_ref, key_ref, value_ref)

    barrier = pltpu.get_barrier_semaphore()
    mates = ({"parts": 1 - part}, {"chan": 1 - chan}, {"rep": 1 - rep})
    for mate in mates:
        pl.semaphore_signal(barrier, inc=1, device_id=mate, device_id_type=MESH)
    for step in range(1, count):
        pl.semaphore_signal(
            barrier, inc=1, device_id={"seq": lax.rem(seq + step, count)}, device_id_type=MESH
        )

    fills = [
        pltpu.make_async_copy(
            tokens_ref,
            all_ref.at[pl.ds(pl.multiple_of(seq * rows, rows), rows),
                       pl.ds(pl.multiple_of((chan * 2 + rep) * columns, columns), columns)],
            fill_sem.at[0])
    ] + [
        pltpu.make_async_copy(
            matrices[m].at[:, own_columns],
            weights_ref.at[pl.ds(pl.multiple_of(seq * depth, depth), depth), pl.ds(m * width, width)],
            fill_sem.at[1 + m])
        for m in range(3)
    ] + [
        pltpu.make_async_copy(source, target, fill_sem.at[4 + n])
        for n, (source, target) in enumerate((
            (rate_hbm, rate_ref), (scale_hbm, scale_ref),
            (residue_hbm, residue_ref), (carried_hbm, carried_ref),
        ))
    ]

    def remote(source, target, send, recv, device):
        return pltpu.make_async_remote_copy(
            src_ref=source, dst_ref=target, send_sem=send, recv_sem=recv,
            device_id=device, device_id_type=MESH,
        )

    def token_block(block, side, core, p):
        top = pl.multiple_of(block * rows + p * piece, piece)
        left = pl.multiple_of((side * 2 + core) * columns, columns)
        return all_ref.at[pl.ds(top, piece), pl.ds(left, columns)]

    def own_piece(p):
        return tokens_ref.at[pl.ds(p * piece, piece), :]

    def hop(block, p, way, source=None):
        here = token_block(block, chan, rep, p)
        return remote(here if source is None else source, here,
                      hop_send.at[block, p, (1 - way) // 2], hop_recv.at[block, p], {"seq": seq + way})

    def side(block, p, source=None):
        here = token_block(block, chan, rep, p)
        return remote(here if source is None else source, here,
                      side_send.at[block, p], side_recv.at[block, p], {"chan": 1 - chan})

    def side_arrival(block, p):
        there = token_block(block, 1 - chan, rep, p)
        return remote(there, there, side_send.at[block, p], side_recv.at[block, p], {"chan": 1 - chan})

    def core(block, which, p, source=None):
        here = token_block(block, chan if which == 0 else 1 - chan, rep, p)
        return remote(here if source is None else source, here,
                      core_send.at[block, which, p], core_recv.at[block, which, p], {"rep": 1 - rep})

    def core_arrival(block, which, p):
        there = token_block(block, chan if which == 0 else 1 - chan, 1 - rep, p)
        return remote(there, there,
                      core_send.at[block, which, p], core_recv.at[block, which, p], {"rep": 1 - rep})

    def weight_block(block, m, part_of):
        top = pl.multiple_of(block * depth + part_of * half, half)
        return weights_ref.at[pl.ds(top, half), pl.ds(m * width, width)]

    def spread(target, m):
        source = matrices[m].at[
            pl.ds(pl.multiple_of(part * half, half), half),
            pl.ds(pl.multiple_of(target * width, width), width),
        ]
        return remote(source, weight_block(seq, m, part),
                      layer_send.at[target, m], layer_recv.at[seq, m], {"seq": target})

    def spread_arrival(block, m):
        here = weight_block(block, m, part)
        return remote(here, here, layer_send.at[block, m], layer_recv.at[block, m], {"seq": block})

    def swap(block, m):
        here = weight_block(block, m, part)
        return remote(here, here, part_send.at[block, m], part_recv.at[block, m], {"parts": 1 - part})

    def swap_arrival(block, m):
        there = weight_block(block, m, 1 - part)
        return remote(there, there, part_send.at[block, m], part_recv.at[block, m], {"parts": 1 - part})

    def result_rows(p):
        return pl.ds(pl.multiple_of(p * piece, piece), piece)

    def result_columns(source):
        return pl.ds(pl.multiple_of(source * width, width), width)

    def gated_rows(block, p):
        return gated_ref.at[pl.ds(pl.multiple_of(block * rows + p * piece, piece), piece), :]

    def give(block, p):
        return remote(gated_rows(block, p), out_ref.at[result_rows(p), result_columns(seq)],
                      out_send.at[block, p], out_recv.at[seq, p], {"seq": block})

    def take(source, p):
        here = out_ref.at[result_rows(p), result_columns(source)]
        return remote(here, here, out_send.at[source, p], out_recv.at[source, p], {"seq": source})

    def keep(p):
        return pltpu.make_async_copy(
            gated_rows(seq, p), out_ref.at[result_rows(p), result_columns(seq)], own_sem.at[p]
        )

    def inside(other):
        return (other >= 0) & (other < count)

    left_total = seq * PIECES
    right_total = (count - 1 - seq) * PIECES

    for fill in fills:
        fill.start()
    pl.semaphore_wait(barrier, count - 1 + len(mates))

    inward = 1 - 2 * ((2 * seq) // count)
    for distance in range(count - 1, 0, -1):
        for other in (seq + inward * distance, seq - inward * distance):
            @pl.when(inside(other))
            def _():
                for m in range(3):
                    spread(other, m).start()
    for p in range(PIECES):
        @pl.when(seq > 0)
        def _():
            hop(seq, p, -1, own_piece(p)).start()

        if p >= PIECES - EARLY:
            @pl.when(seq + 1 < count)
            def _():
                hop(seq, p, 1, own_piece(p)).start()
        else:
            @pl.when(seq == 0)
            def _():
                hop(seq, p, 1, own_piece(p)).start()
        side(seq, p, own_piece(p)).start()
        core(seq, 0, p, own_piece(p)).start()
    for p in range(PIECES):
        side_arrival(seq, p).wait_recv()
        core(seq, 1, p).start()
    for distance in range(1, count):
        for m in range(3):
            for other in (seq - distance, seq + distance):
                @pl.when(inside(other))
                def _():
                    spread_arrival(other, m).wait_recv()
                    swap(other, m).start()
    for fill in fills:
        fill.wait()

    lane_groups = width // LANES
    chunk = piece // CHUNKS

    def project(block, p):
        for which in range(2):
            core_arrival(block, which, p).wait_recv()
        top = pl.ds(pl.multiple_of(block * rows + p * piece, piece), piece)
        found = jnp.dot(all_ref[top, :], weights_ref[...], preferred_element_type=jnp.float32)
        found = found.astype(jnp.bfloat16)
        query_rows[top, :] = found[:, :width]
        product = (
            found[:, width : 2 * width].astype(jnp.float32) * found[:, 2 * width :].astype(jnp.float32)
        )
        product = product.astype(jnp.bfloat16).astype(jnp.float32)
        for group in range(lane_groups):
            signal[group, top, :] = product[:, group * LANES : (group + 1) * LANES]

    def scan(g, _):
        block, p = g // PIECES, lax.rem(g, PIECES)
        top = pl.multiple_of(g * piece, piece)
        for group in range(lane_groups):
            lanes = pl.ds(group * LANES, LANES)
            rates = rate_ref[:, lanes]
            residues = residue_ref[:, lanes]
            scale = scale_ref[:, lanes]
            decay = jnp.exp(-rates)
            weight = residues * scale
            chunk_decay = jnp.exp(-rates * chunk)

            def rows_of(array):
                return [jnp.broadcast_to(array[m : m + 1, :], (CHUNKS, LANES)) for m in range(modes)]

            decays = rows_of(decay)
            weights = rows_of(weight)

            def sums(step, states):
                here = signal[group, pl.ds(top + step, CHUNKS, stride=chunk), :]
                return tuple(d * s + here for d, s in zip(decays, states))

            zero = jnp.zeros((CHUNKS, LANES), jnp.float32)
            finals = lax.fori_loop(0, chunk, sums, (zero,) * modes, unroll=4)
            for m in range(modes):
                ends[m] = finals[m]
            state = carried_ref[:, lanes]
            for c in range(CHUNKS):
                entering[:, c, :] = residues * state
                state = chunk_decay * state + scale * ends[:, c, :]
            carried_ref[:, lanes] = state

            def outputs(step, states):
                here = signal[group, pl.ds(top + step, CHUNKS, stride=chunk), :]
                states = tuple(d * s + w * here for d, s, w in zip(decays, states, weights))
                terms = list(states)
                while len(terms) > 1:
                    terms = [a + b for a, b in zip(terms[::2], terms[1::2])] + (
                        [terms[-1]] if len(terms) % 2 else []
                    )
                conv[group, pl.ds(step, CHUNKS, stride=chunk), :] = terms[0]
                return states

            starts = tuple(entering[m] for m in range(modes))
            lax.fori_loop(0, chunk, outputs, starts, unroll=4)
            rounded = conv[group].astype(jnp.bfloat16).astype(jnp.float32)
            gated_ref[pl.ds(top, piece), lanes] = (
                query_rows[pl.ds(top, piece), lanes].astype(jnp.float32) * rounded
            ).astype(jnp.bfloat16)

        @pl.when(block == seq)
        def _():
            keep(p).start()

        @pl.when(block != seq)
        def _():
            give(block, p).start()

        return 0

    def left_of(i):
        return i // PIECES, lax.rem(i, PIECES)

    def right_of(i):
        return seq + 1 + i // PIECES, lax.rem(i, PIECES)

    def scanned(n):
        reach = jnp.maximum(seq, 1) * PIECES
        whole = jnp.minimum((seq + 1) * PIECES + n, count * PIECES)
        return jnp.where(n < reach, n, whole)

    def slot(k, _):
        @pl.when(k < left_total)
        def _():
            block, p = left_of(k)
            hop(block, p, 1).wait_recv()

            @pl.when(seq + 1 < count)
            def _():
                hop(block, p, 1).start()

            side(block, p).start()
            core(block, 0, p).start()

            @pl.when((k == left_total - 1) & (seq + 1 < count))
            def _():
                for q in range(PIECES - EARLY):
                    hop(seq, q, 1, own_piece(q)).start()

        @pl.when(k < right_total)
        def _():
            block, p = right_of(k)
            hop(block, p, -1).wait_recv()

            @pl.when(seq > 0)
            def _():
                hop(block, p, -1).start()

            side(block, p).start()
            core(block, 0, p).start()

        before = k - 1

        @pl.when((before >= 0) & (before < left_total))
        def _():
            block, p = left_of(before)
            side_arrival(block, p).wait_recv()
            core(block, 1, p).start()

        @pl.when((before >= 0) & (before < right_total))
        def _():
            block, p = right_of(before)
            side_arrival(block, p).wait_recv()
            core(block, 1, p).start()

        @pl.when(k == 2)
        def _():
            for distance in range(1, count):
                for other in (seq - distance, seq + distance):
                    @pl.when(inside(other))
                    def _():
                        for m in range(3):
                            swap_arrival(other, m).wait_recv()

        @pl.when(k >= 2)
        def _():
            n = k - 2

            def one(which, _):
                block = jnp.where(which == 0, n // PIECES,
                                  jnp.where(which == 1, seq + 1 + n // PIECES, seq))
                limit = jnp.where(which == 0, left_total,
                                  jnp.where(which == 1, right_total, PIECES))

                @pl.when(n < limit)
                def _():
                    project(block, lax.rem(n, PIECES))

                return 0

            lax.fori_loop(0, 3, one, 0)
            lax.fori_loop(scanned(n), scanned(n + 1), scan, 0)

        return 0

    lax.fori_loop(0, (count - 1) * PIECES + 2, slot, 0)
    state_ref[...] = carried_ref[...]

    for p in range(PIECES):
        keep(p).wait()
        @pl.when(seq > 0)
        def _():
            hop(seq, p, -1, own_piece(p)).wait_send()

        @pl.when(seq + 1 < count)
        def _():
            hop(seq, p, 1, own_piece(p)).wait_send()

        side(seq, p, own_piece(p)).wait_send()
        core(seq, 0, p, own_piece(p)).wait_send()
        core(seq, 1, p).wait_send()
    for distance in range(1, count):
        for other, way in ((seq - distance, 1), (seq + distance, -1)):
            @pl.when(inside(other))
            def _():
                for p in range(PIECES):
                    @pl.when(inside(seq + way))
                    def _():
                        hop(other, p, way).wait_send()

                    side(other, p).wait_send()
                    for which in range(2):
                        core(other, which, p).wait_send()
                    give(other, p).wait_send()
                    take(other, p).wait_recv()
                for m in range(3):
                    spread(other, m).wait_send()
                    swap(other, m).wait_send()


def whole_layer(tokens, w_query, w_key, w_value, rate, residue, carried, count):
    rows, columns = tokens.shape
    depth, outer = w_query.shape
    width, modes = rate.shape
    length = rows * count
    vmem = pl.BlockSpec(memory_space=pltpu.VMEM)
    anywhere = pl.BlockSpec(memory_space=pl.ANY)
    dma = pltpu.SemaphoreType.DMA
    table = pltpu.VMEM((modes, width), jnp.float32)
    gated, state = pl.pallas_call(
        functools.partial(layer_kernel, count),
        out_shape=(
            jax.ShapeDtypeStruct((rows, outer), jnp.bfloat16),
            jax.ShapeDtypeStruct((modes, width), jnp.float32),
        ),
        in_specs=[anywhere] * 8,
        out_specs=(anywhere, vmem),
        scratch_shapes=[
            pltpu.VMEM((length, columns * 4), jnp.bfloat16),
            pltpu.VMEM((depth * count, 3 * width), jnp.bfloat16),
            pltpu.VMEM((length, width), jnp.bfloat16),
            pltpu.VMEM((width // LANES, length, LANES), jnp.float32),
            pltpu.VMEM((width // LANES, rows // PIECES, LANES), jnp.float32),
            pltpu.VMEM((length, width), jnp.bfloat16),
            pltpu.VMEM((modes, CHUNKS, LANES), jnp.float32),
            pltpu.VMEM((modes, CHUNKS, LANES), jnp.float32),
        ] + [table] * 4 + [
            dma((8,)),
            dma((count, PIECES, 2)), dma((count, PIECES)),
            dma((count, PIECES)), dma((count, PIECES)),
            dma((count, 2, PIECES)), dma((count, 2, PIECES)),
            dma((count, 3)), dma((count, 3)),
            dma((count, 3)), dma((count, 3)),
            dma((count, PIECES)), dma((count, PIECES)),
            dma((PIECES,)),
        ],
        compiler_params=pltpu.CompilerParams(
            collective_id=0, has_side_effects=True, vmem_limit_bytes=60 * 2**20
        ),
    )(tokens, w_query, w_key, w_value, rate.T, mode_scale(rate).T, residue.T, carried.T)
    return gated, state.T


def per_device_channels(tokens, w_query, w_key, w_value, decay_rate, residue, carried):
    count = lax.axis_size("seq")
    return whole_layer(tokens, w_query, w_key, w_value, decay_rate, residue, carried, count)


def solution(mesh):
    in_specs = (
        P(("parts", "seq"), ("chan", "rep")),
        P("seq", ("chan", "rep")),
        P("seq", ("chan", "rep")),
        P("seq", ("chan", "rep")),
        P(("chan", "rep", "seq"), None),
        P(("chan", "rep", "seq"), None),
        P(("parts", "chan", "rep", "seq"), None),
    )
    out_specs = (P(("parts", "seq"), ("chan", "rep")), P(("parts", "chan", "rep", "seq"), None))

    def body(*arrays):
        own_channels = arrays[4].shape[0]
        mates = all(mesh.shape[a] == 2 for a in ("parts", "chan", "rep"))
        chosen = per_device_channels if own_channels % LANES == 0 and mates else per_device
        return chosen(*arrays)

    return jax.shard_map(body, mesh=mesh, in_specs=in_specs, out_specs=out_specs, check_vma=False)
```

time: 186 us -> 212 us (1.14)
  Pallas kernels: 180 us -> 207 us
    pallas_call x2 -> x1, Pallas kernels: 180 us -> 207 us  [whole_layer(): pl.pallas_call(functools.partial(layer_kernel, count), out_shape=(jax.Sha...]
where the time goes in v1:
time: 212 us
  Pallas kernels  207 us (98%)
  local copies, waits for them, and re-layouts  2.88 us (1%)
    pallas_call x1, Pallas kernels, whole_layer(): pl.pallas_call(functools.partial(layer_kernel, count), out_shape=(jax.Sha...  207 us

profile of v1, /device:TPU:25, one launch (start us, length us, event | category | flops | bytes accessed | tf_op | source)
XLA Modules:
  0.0 211.9 jit_solution(1796757104121182896)
XLA Ops:
  0.6 1.3 sqrt_bitcast_fusion.scale_hbm
  2.0 207.0 %shard_map.86 = (bf16[512,1024]{1,0:T(8,128)(2,1)}, f32[16,256]{1,0:T(8,128)}) custom-call(bf16[512,1024]{1,0:T(8,128)(2,1)} %tokens_ref.1, bf16[1024,1024]{1,0:T(8,128)(2,1)} %query_ref.1, bf16[1024,1024]{1,0:T(8,128)(2,1)} %key_ref.1, bf16[1024,1024]{1,0:T(8,128)(2,1)} %value_ref.1, f32[16,256]{1,0:T(8,128)} %bitcast.6, ...), custom_call_target="tpu_custom_call" | custom-call | tf_op jit(solution)/shard_map/pallas_call | solution.py:494
  209.0 0.0 copy-start
  209.0 2.3 %copy.11 = bf16[512,1024]{1,0:T(8,128)(2,1)} copy(bf16[512,1024]{1,0:T(8,128)(2,1)} %get-tuple-element.8) | data formatting | bytes 2097152
  211.3 0.0 copy-done
  211.3 0.6 copy.12
Async XLA Ops:
  209.0 2.3 %copy-start = (f32[16,256]{1,0:T(8,128)S(1)}, f32[16,256]{1,0:T(8,128)}, u32[]{:S(2)}) copy-start(f32[16,256]{1,0:T(8,128)} %get-tuple-element.5) | copy-start | bytes 49156

commit v2 on v1

--- a/solution.py
+++ b/solution.py
@@ -108,7 +108,39 @@
 
 
 PIECES = 4
-EARLY = 2
+SIDE_LAG = 2
+LAG = 3
+LEFT_HOLD = 1
+RIGHT_HOLD = 0
+
+
+def block_orders(count):
+    if count == 4:
+        return ((1, 2, 3), (0, 2, 3), (3, 0, 1), (2, 0, 1))
+    return tuple(
+        tuple(sorted((b for b in range(count) if b != z), key=lambda b: (abs(b - z), b)))
+        for z in range(count)
+    )
+
+
+def reach_table(orders):
+    count = len(orders)
+    last = (count - 1) * PIECES
+    table = []
+    for z, order in enumerate(orders):
+        when = {}
+        for p in range(PIECES):
+            when[z, p] = when[order[0], p] = PIECES + p
+            for n in range(1, count - 1):
+                when[order[n], p] = n * PIECES + p + LAG
+        row = [0]
+        for k in range(PIECES, last + LAG):
+            g = row[-1]
+            while g < count * PIECES and when[divmod(g, PIECES)] <= k:
+                g += 1
+            row.append(g)
+        table.append(row)
+    return table
 
 
 def layer_kernel(count, tokens_ref, query_ref, key_ref, value_ref, rate_hbm, scale_hbm, residue_hbm,
@@ -243,45 +275,111 @@
     def inside(other):
         return (other >= 0) & (other < count)
 
-    left_total = seq * PIECES
-    right_total = (count - 1 - seq) * PIECES
+    def pick(values, index):
+        found = values[0]
+        for n in range(1, len(values)):
+            found = jnp.where(index == n, values[n], found)
+        return found
+
+    def by_plane(table, index):
+        flat = [value for row in table for value in row]
+        return pick(flat, seq * len(table[0]) + index)
+
+    orders = block_orders(count)
+    ready = reach_table(orders)
+    is_first, is_last = seq == 0, seq == count - 1
+    is_end = is_first | is_last
+    deferred = (seq == 1) if count == 4 else (seq == count)
 
     for fill in fills:
         fill.start()
     pl.semaphore_wait(barrier, count - 1 + len(mates))
 
-    inward = 1 - 2 * ((2 * seq) // count)
-    for distance in range(count - 1, 0, -1):
-        for other in (seq + inward * distance, seq - inward * distance):
+    def send_weights(way, distances):
+        for distance in distances:
+            other = seq + way * distance
+
             @pl.when(inside(other))
             def _():
                 for m in range(3):
                     spread(other, m).start()
+
+    def send_own(way):
+        for p in range(PIECES):
+            hop(seq, p, way, own_piece(p)).start()
+
     for p in range(PIECES):
-        @pl.when(seq > 0)
-        def _():
-            hop(seq, p, -1, own_piece(p)).start()
-
-        if p >= PIECES - EARLY:
-            @pl.when(seq + 1 < count)
-            def _():
-                hop(seq, p, 1, own_piece(p)).start()
-        else:
-            @pl.when(seq == 0)
-            def _():
-                hop(seq, p, 1, own_piece(p)).start()
         side(seq, p, own_piece(p)).start()
         core(seq, 0, p, own_piece(p)).start()
-    for p in range(PIECES):
-        side_arrival(seq, p).wait_recv()
-        core(seq, 1, p).start()
-    for distance in range(1, count):
+    for way in (1, -1):
+        @pl.when(inside(seq + way))
+        def _():
+            send_weights(way, range(count - 1, 0, -1))
+            if way == 1:
+                @pl.when(jnp.logical_not(deferred))
+                def _():
+                    send_own(way)
+            else:
+                send_own(way)
+
+    def relay(block, p):
+        way = jnp.where(block < seq, 1, -1)
+        hop(block, p, way).wait_recv()
+
+        @pl.when(inside(seq + way))
+        def _():
+            hop(block, p, way).start()
+
+        side(block, p).start()
+        core(block, 0, p).start()
+
+    def pass_side(block, p):
+        side_arrival(block, p).wait_recv()
+        core(block, 1, p).start()
+
+    def pass_weights(other, m):
+        @pl.when(inside(other))
+        def _():
+            spread_arrival(other, m).wait_recv()
+            swap(other, m).start()
+
+    toward = jnp.where(2 * seq < count, -1, 1)
+    first_block = by_plane(orders, 0)
+
+    @pl.when(is_end)
+    def _():
         for m in range(3):
-            for other in (seq - distance, seq + distance):
-                @pl.when(inside(other))
-                def _():
-                    spread_arrival(other, m).wait_recv()
-                    swap(other, m).start()
+            pass_side(seq, m)
+            pass_weights(seq - toward * (count - 1), m)
+        for p in range(3, PIECES):
+            pass_side(seq, p)
+        for distance in range(1, count - 1):
+            for m in range(3):
+                pass_weights(seq - toward * distance, m)
+        for p in range(PIECES):
+            relay(first_block, p)
+
+    @pl.when(jnp.logical_not(is_end))
+    def _():
+        for p in range(PIECES):
+            pass_side(seq, p)
+        for distance in range(count - 2, 1, -1):
+            for m in range(3):
+                pass_weights(seq - toward * distance, m)
+        for distance in range(count - 2, 0, -1):
+            for m in range(3):
+                pass_weights(seq + toward * distance, m)
+        for p in range(PIECES):
+            relay(first_block, p)
+            if p < 3:
+                pass_weights(seq - toward, p)
+
+        @pl.when(deferred)
+        def _():
+            send_own(1)
+
+    for p in range(PIECES - SIDE_LAG):
+        pass_side(first_block, p)
     for fill in fills:
         fill.wait()
 
@@ -356,68 +454,43 @@
         def _():
             keep(p).start()
 
-        @pl.when(block != seq)
-        def _():
-            give(block, p).start()
-
         return 0
 
-    def left_of(i):
-        return i // PIECES, lax.rem(i, PIECES)
-
-    def right_of(i):
-        return seq + 1 + i // PIECES, lax.rem(i, PIECES)
-
-    def scanned(n):
-        reach = jnp.maximum(seq, 1) * PIECES
-        whole = jnp.minimum((seq + 1) * PIECES + n, count * PIECES)
-        return jnp.where(n < reach, n, whole)
+    def scan_and_send(g, k):
+        scan(g, 0)
+
+        block = g // PIECES
+
+        @pl.when((block != seq) & (k >= release(block)))
+        def _():
+            give(block, lax.rem(g, PIECES)).start()
+
+        return k
+
+    def release(block):
+        later = jnp.where(block < seq, last + LEFT_HOLD, last + RIGHT_HOLD)
+        return jnp.where(is_end & ((block == seq - 1) | (block == seq + 1)), 0, later)
+
+    def send_held(g, k):
+        block = g // PIECES
+
+        @pl.when((block != seq) & (release(block) == k))
+        def _():
+            give(block, lax.rem(g, PIECES)).start()
+
+        return k
+
+    last = (count - 1) * PIECES
+
+    def block_of(k):
+        return by_plane(orders, k // PIECES)
 
     def slot(k, _):
-        @pl.when(k < left_total)
-        def _():
-            block, p = left_of(k)
-            hop(block, p, 1).wait_recv()
-
-            @pl.when(seq + 1 < count)
-            def _():
-                hop(block, p, 1).start()
-
-            side(block, p).start()
-            core(block, 0, p).start()
-
-            @pl.when((k == left_total - 1) & (seq + 1 < count))
-            def _():
-                for q in range(PIECES - EARLY):
-                    hop(seq, q, 1, own_piece(q)).start()
-
-        @pl.when(k < right_total)
-        def _():
-            block, p = right_of(k)
-            hop(block, p, -1).wait_recv()
-
-            @pl.when(seq > 0)
-            def _():
-                hop(block, p, -1).start()
-
-            side(block, p).start()
-            core(block, 0, p).start()
-
-        before = k - 1
-
-        @pl.when((before >= 0) & (before < left_total))
-        def _():
-            block, p = left_of(before)
-            side_arrival(block, p).wait_recv()
-            core(block, 1, p).start()
-
-        @pl.when((before >= 0) & (before < right_total))
-        def _():
-            block, p = right_of(before)
-            side_arrival(block, p).wait_recv()
-            core(block, 1, p).start()
-
-        @pl.when(k == 2)
+        @pl.when(k < last)
+        def _():
+            relay(block_of(k), lax.rem(k, PIECES))
+
+        @pl.when(k == PIECES)
         def _():
             for distance in range(1, count):
                 for other in (seq - distance, seq + distance):
@@ -426,28 +499,33 @@
                         for m in range(3):
                             swap_arrival(other, m).wait_recv()
 
-        @pl.when(k >= 2)
-        def _():
-            n = k - 2
-
-            def one(which, _):
-                block = jnp.where(which == 0, n // PIECES,
-                                  jnp.where(which == 1, seq + 1 + n // PIECES, seq))
-                limit = jnp.where(which == 0, left_total,
-                                  jnp.where(which == 1, right_total, PIECES))
-
-                @pl.when(n < limit)
-                def _():
-                    project(block, lax.rem(n, PIECES))
-
-                return 0
-
-            lax.fori_loop(0, 3, one, 0)
-            lax.fori_loop(scanned(n), scanned(n + 1), scan, 0)
+        def one(which, _):
+            early = which < 2
+            n = jnp.where(early, k - PIECES, k - LAG)
+            block = jnp.where(which == 0, seq, jnp.where(which == 1, first_block, block_of(k - LAG)))
+            known = (early & (n < PIECES)) | (jnp.logical_not(early) & (n >= PIECES))
+
+            @pl.when(known)
+            def _():
+                project(block, lax.rem(n, PIECES))
+
+            return 0
+
+        lax.fori_loop(0, 3, one, 0)
+        done, reach = by_plane(ready, k - PIECES), by_plane(ready, k - PIECES + 1)
+        lax.fori_loop(done, reach, scan_and_send, k)
+
+        @pl.when((k == last + LEFT_HOLD) | (k == last + RIGHT_HOLD))
+        def _():
+            lax.fori_loop(0, done, send_held, k)
+
+        @pl.when(k < last + SIDE_LAG)
+        def _():
+            pass_side(block_of(k - SIDE_LAG), lax.rem(k - SIDE_LAG, PIECES))
 
         return 0
 
-    lax.fori_loop(0, (count - 1) * PIECES + 2, slot, 0)
+    lax.fori_loop(PIECES, last + LAG, slot, 0)
     state_ref[...] = carried_ref[...]
 
     for p in range(PIECES):

time: 212 us -> 160 us (0.75)
  Pallas kernels: 207 us -> 153 us
    pallas_call x1, Pallas kernels: 207 us -> 153 us  [whole_layer(): pl.pallas_call(functools.partial(layer_kernel, count), out_shape=(jax.Sha...]
where the time goes in v2:
time: 160 us; the launch traced here: 158 us
  Pallas kernels  153 us (96%)
  local copies, waits for them, and re-layouts  2.88 us (2%)
    pallas_call x1, Pallas kernels, whole_layer(): pl.pallas_call(functools.partial(layer_kernel, count), out_shape=(jax.Sha...  153 us

profile of v2, /device:TPU:25, one launch (start us, length us, event | category | flops | bytes accessed | tf_op | source)
XLA Modules:
  0.0 158.1 jit_solution(7617643946479446342)
XLA Ops:
  0.6 1.3 sqrt_bitcast_fusion.scale_hbm
  2.0 153.3 %shard_map.86 = (bf16[512,1024]{1,0:T(8,128)(2,1)}, f32[16,256]{1,0:T(8,128)}) custom-call(bf16[512,1024]{1,0:T(8,128)(2,1)} %tokens_ref.1, bf16[1024,1024]{1,0:T(8,128)(2,1)} %query_ref.1, bf16[1024,1024]{1,0:T(8,128)(2,1)} %key_ref.1, bf16[1024,1024]{1,0:T(8,128)(2,1)} %value_ref.1, f32[16,256]{1,0:T(8,128)} %bitcast.6, ...), custom_call_target="tpu_custom_call" | custom-call | tf_op jit(solution)/shard_map/pallas_call | solution.py:572
  155.2 0.0 copy-start
  155.3 2.3 %copy.11 = bf16[512,1024]{1,0:T(8,128)(2,1)} copy(bf16[512,1024]{1,0:T(8,128)(2,1)} %get-tuple-element.8) | data formatting | bytes 2097152
  157.5 0.0 copy-done
  157.5 0.6 copy.12
Async XLA Ops:
  155.2 2.3 %copy-start = (f32[16,256]{1,0:T(8,128)S(1)}, f32[16,256]{1,0:T(8,128)}, u32[]{:S(2)}) copy-start(f32[16,256]{1,0:T(8,128)} %get-tuple-element.5) | copy-start | bytes 49156

commit v3 on v2

--- a/solution.py
+++ b/solution.py
@@ -110,8 +110,7 @@
 PIECES = 4
 SIDE_LAG = 2
 LAG = 3
-LEFT_HOLD = 1
-RIGHT_HOLD = 0
+CAP = 2
 
 
 def block_orders(count):
@@ -120,6 +119,25 @@
     return tuple(
         tuple(sorted((b for b in range(count) if b != z), key=lambda b: (abs(b - z), b)))
         for z in range(count)
+    )
+
+
+def one_less_exp(x):
+    series = jnp.ones_like(x)
+    for n in range(9, 1, -1):
+        series = 1.0 - series * x * (1.0 / n)
+    return jnp.where(x < 0.25, x * series, 1.0 - jnp.exp(-x))
+
+
+def release_table(count):
+    if count != 4:
+        return ((0,) * count,) * count
+    last = (count - 1) * PIECES
+    return (
+        (0, 0, last - 2, 0),
+        (last, 0, 0, last),
+        (last, 0, 0, last),
+        (last - 1, 0, 0, 0),
     )
 
 
@@ -136,14 +154,15 @@
         row = [0]
         for k in range(PIECES, last + LAG):
             g = row[-1]
-            while g < count * PIECES and when[divmod(g, PIECES)] <= k:
+            top = g + CAP if k < last else count * PIECES
+            while g < min(top, count * PIECES) and when[divmod(g, PIECES)] <= k:
                 g += 1
             row.append(g)
         table.append(row)
     return table
 
 
-def layer_kernel(count, tokens_ref, query_ref, key_ref, value_ref, rate_hbm, scale_hbm, residue_hbm,
+def layer_kernel(count, tokens_ref, query_ref, key_ref, value_ref, rate_hbm, residue_hbm,
                  carried_hbm, out_ref, state_ref,
                  all_ref, weights_ref, query_rows, signal, conv, gated_ref, ends, entering,
                  rate_ref, scale_ref, residue_ref, carried_ref,
@@ -183,8 +202,7 @@
     ] + [
         pltpu.make_async_copy(source, target, fill_sem.at[4 + n])
         for n, (source, target) in enumerate((
-            (rate_hbm, rate_ref), (scale_hbm, scale_ref),
-            (residue_hbm, residue_ref), (carried_hbm, carried_ref),
+            (rate_hbm, rate_ref), (residue_hbm, residue_ref), (carried_hbm, carried_ref),
         ))
     ]
 
@@ -308,9 +326,6 @@
         for p in range(PIECES):
             hop(seq, p, way, own_piece(p)).start()
 
-    for p in range(PIECES):
-        side(seq, p, own_piece(p)).start()
-        core(seq, 0, p, own_piece(p)).start()
     for way in (1, -1):
         @pl.when(inside(seq + way))
         def _():
@@ -321,6 +336,10 @@
                     send_own(way)
             else:
                 send_own(way)
+
+    for p in range(PIECES):
+        side(seq, p, own_piece(p)).start()
+        core(seq, 0, p, own_piece(p)).start()
 
     def relay(block, p):
         way = jnp.where(block < seq, 1, -1)
@@ -383,6 +402,7 @@
     for fill in fills:
         fill.wait()
 
+    scale_ref[...] = jnp.sqrt(one_less_exp(2.0 * rate_ref[...]))
     lane_groups = width // LANES
     chunk = piece // CHUNKS
 
@@ -467,9 +487,10 @@
 
         return k
 
+    releases = release_table(count)
+
     def release(block):
-        later = jnp.where(block < seq, last + LEFT_HOLD, last + RIGHT_HOLD)
-        return jnp.where(is_end & ((block == seq - 1) | (block == seq + 1)), 0, later)
+        return by_plane(releases, block)
 
     def send_held(g, k):
         block = g // PIECES
@@ -515,7 +536,7 @@
         done, reach = by_plane(ready, k - PIECES), by_plane(ready, k - PIECES + 1)
         lax.fori_loop(done, reach, scan_and_send, k)
 
-        @pl.when((k == last + LEFT_HOLD) | (k == last + RIGHT_HOLD))
+        @pl.when(k >= last - 2)
         def _():
             lax.fori_loop(0, done, send_held, k)
 
@@ -529,7 +550,6 @@
     state_ref[...] = carried_ref[...]
 
     for p in range(PIECES):
-        keep(p).wait()
         @pl.when(seq > 0)
         def _():
             hop(seq, p, -1, own_piece(p)).wait_send()
@@ -541,23 +561,37 @@
         side(seq, p, own_piece(p)).wait_send()
         core(seq, 0, p, own_piece(p)).wait_send()
         core(seq, 1, p).wait_send()
-    for distance in range(1, count):
-        for other, way in ((seq - distance, 1), (seq + distance, -1)):
-            @pl.when(inside(other))
-            def _():
-                for p in range(PIECES):
-                    @pl.when(inside(seq + way))
-                    def _():
-                        hop(other, p, way).wait_send()
-
-                    side(other, p).wait_send()
-                    for which in range(2):
-                        core(other, which, p).wait_send()
-                    give(other, p).wait_send()
-                    take(other, p).wait_recv()
-                for m in range(3):
-                    spread(other, m).wait_send()
-                    swap(other, m).wait_send()
+    others = [
+        (other, way)
+        for distance in range(1, count)
+        for other, way in ((seq - distance, 1), (seq + distance, -1))
+    ]
+    for other, way in others:
+        @pl.when(inside(other))
+        def _():
+            for m in range(3):
+                spread(other, m).wait_send()
+                swap(other, m).wait_send()
+            for p in range(PIECES):
+                @pl.when(inside(seq + way))
+                def _():
+                    hop(other, p, way).wait_send()
+
+                side(other, p).wait_send()
+                for which in range(2):
+                    core(other, which, p).wait_send()
+    for p in range(PIECES):
+        keep(p).wait()
+    for other, way in others:
+        @pl.when(inside(other))
+        def _():
+            for p in range(PIECES):
+                give(other, p).wait_send()
+    for other, way in others:
+        @pl.when(inside(other))
+        def _():
+            for p in range(PIECES):
+                take(other, p).wait_recv()
 
 
 def whole_layer(tokens, w_query, w_key, w_value, rate, residue, carried, count):
@@ -569,13 +603,14 @@
     anywhere = pl.BlockSpec(memory_space=pl.ANY)
     dma = pltpu.SemaphoreType.DMA
     table = pltpu.VMEM((modes, width), jnp.float32)
+    operands = (tokens, w_query, w_key, w_value, rate.T, residue.T, carried.T)
     gated, state = pl.pallas_call(
         functools.partial(layer_kernel, count),
         out_shape=(
             jax.ShapeDtypeStruct((rows, outer), jnp.bfloat16),
             jax.ShapeDtypeStruct((modes, width), jnp.float32),
         ),
-        in_specs=[anywhere] * 8,
+        in_specs=[anywhere] * 7,
         out_specs=(anywhere, vmem),
         scratch_shapes=[
             pltpu.VMEM((length, columns * 4), jnp.bfloat16),
@@ -587,7 +622,7 @@
             pltpu.VMEM((modes, CHUNKS, LANES), jnp.float32),
             pltpu.VMEM((modes, CHUNKS, LANES), jnp.float32),
         ] + [table] * 4 + [
-            dma((8,)),
+            dma((7,)),
             dma((count, PIECES, 2)), dma((count, PIECES)),
             dma((count, PIECES)), dma((count, PIECES)),
             dma((count, 2, PIECES)), dma((count, 2, PIECES)),
@@ -597,9 +632,9 @@
             dma((PIECES,)),
         ],
         compiler_params=pltpu.CompilerParams(
-            collective_id=0, has_side_effects=True, vmem_limit_bytes=60 * 2**20
+            collective_id=0, has_side_effects=True, vmem_limit_bytes=40 * 2**20
         ),
-    )(tokens, w_query, w_key, w_value, rate.T, mode_scale(rate).T, residue.T, carried.T)
+    )(*(pltpu.with_memory_space_constraint(array, pltpu.HBM) for array in operands))
     return gated, state.T
 
 

time: 160 us -> 150 us (0.938)
  Pallas kernels: 153 us -> 146 us
    pallas_call x1, Pallas kernels: 153 us -> 146 us  [whole_layer(): pl.pallas_call(functools.partial(layer_kernel, count), out_shape=(jax.Sha...]
where the time goes in v3:
time: 150 us; the launch traced here: 149 us
  Pallas kernels  146 us (97%)
  local copies, waits for them, and re-layouts  1.58 us (1%)
    pallas_call x1, Pallas kernels, whole_layer(): pl.pallas_call(functools.partial(layer_kernel, count), out_shape=(jax.Sha...  146 us

profile of v3, /device:TPU:25, one launch (start us, length us, event | category | flops | bytes accessed | tf_op | source)
XLA Modules:
  0.0 148.7 jit_solution(18209648531023537299)
XLA Ops:
  0.6 146.5 %shard_map.86 = (bf16[512,1024]{1,0:T(8,128)(2,1)S(1)}, f32[16,256]{1,0:T(8,128)S(1)}) custom-call(bf16[512,1024]{1,0:T(8,128)(2,1)} %tokens_ref.1, bf16[1024,1024]{1,0:T(8,128)(2,1)} %query_ref.1, bf16[1024,1024]{1,0:T(8,128)(2,1)} %key_ref.1, bf16[1024,1024]{1,0:T(8,128)(2,1)} %value_ref.1, f32[16,256]{1,0:T(8,128)} %bitcast.5, f32[16,256]{1,0:T(8,128)} %bitcast.6, ...), custom_call_target="tpu_custom_call" | custom-call | tf_op jit(solution)/shard_map/pallas_call | solution.py:607
  147.1 1.0 copy.11
  148.1 0.6 copy.12

commit v4 on v3

--- a/solution.py
+++ b/solution.py
@@ -108,9 +108,10 @@
 
 
 PIECES = 4
-SIDE_LAG = 2
-LAG = 3
+SIDE_LAG = (1, 2)
+LAG = (2, 3)
 CAP = 2
+UNROLL = 8
 
 
 def block_orders(count):
@@ -135,8 +136,8 @@
     last = (count - 1) * PIECES
     return (
         (0, 0, last - 2, 0),
-        (last, 0, 0, last),
-        (last, 0, 0, last),
+        (last - 1, 0, 0, last - 1),
+        (last, 0, 0, last - 1),
         (last - 1, 0, 0, 0),
     )
 
@@ -150,9 +151,9 @@
         for p in range(PIECES):
             when[z, p] = when[order[0], p] = PIECES + p
             for n in range(1, count - 1):
-                when[order[n], p] = n * PIECES + p + LAG
+                when[order[n], p] = n * PIECES + p + LAG[0 if z in (0, count - 1) else 1]
         row = [0]
-        for k in range(PIECES, last + LAG):
+        for k in range(PIECES, last + LAG[1]):
             g = row[-1]
             top = g + CAP if k < last else count * PIECES
             while g < min(top, count * PIECES) and when[divmod(g, PIECES)] <= k:
@@ -165,7 +166,7 @@
 def layer_kernel(count, tokens_ref, query_ref, key_ref, value_ref, rate_hbm, residue_hbm,
                  carried_hbm, out_ref, state_ref,
                  all_ref, weights_ref, query_rows, signal, conv, gated_ref, ends, entering,
-                 rate_ref, scale_ref, residue_ref, carried_ref,
+                 rate_ref, scale_ref, residue_ref, carried_ref, decay_ref, weight_ref, step_ref,
                  fill_sem, hop_send, hop_recv, side_send, side_recv, core_send, core_recv,
                  part_send, part_recv, layer_send, layer_recv, out_send, out_recv, own_sem):
     part, seq, chan, rep = (lax.axis_index(a) for a in ("parts", "seq", "chan", "rep"))
@@ -223,26 +224,38 @@
     def hop(block, p, way, source=None):
         here = token_block(block, chan, rep, p)
         return remote(here if source is None else source, here,
-                      hop_send.at[block, p, (1 - way) // 2], hop_recv.at[block, p], {"seq": seq + way})
+                      hop_send.at[block, (1 - way) // 2], hop_recv.at[block, p], {"seq": seq + way})
 
     def side(block, p, source=None):
         here = token_block(block, chan, rep, p)
         return remote(here if source is None else source, here,
-                      side_send.at[block, p], side_recv.at[block, p], {"chan": 1 - chan})
+                      side_send.at[block], side_recv.at[block, p], {"chan": 1 - chan})
 
     def side_arrival(block, p):
         there = token_block(block, 1 - chan, rep, p)
-        return remote(there, there, side_send.at[block, p], side_recv.at[block, p], {"chan": 1 - chan})
+        return remote(there, there, side_send.at[block], side_recv.at[block, p], {"chan": 1 - chan})
 
     def core(block, which, p, source=None):
         here = token_block(block, chan if which == 0 else 1 - chan, rep, p)
         return remote(here if source is None else source, here,
-                      core_send.at[block, which, p], core_recv.at[block, which, p], {"rep": 1 - rep})
-
-    def core_arrival(block, which, p):
-        there = token_block(block, chan if which == 0 else 1 - chan, 1 - rep, p)
-        return remote(there, there,
-                      core_send.at[block, which, p], core_recv.at[block, which, p], {"rep": 1 - rep})
+                      core_send.at[block], core_recv.at[block, p], {"rep": 1 - rep})
+
+    def core_arrivals(block, p):
+        top = pl.multiple_of(block * rows + p * piece, piece)
+        there = all_ref.at[pl.ds(top, piece), pl.ds(0, 2 * columns)]
+        return remote(there, there, core_send.at[block], core_recv.at[block, p], {"rep": 1 - rep})
+
+    def sent(semaphore, other, wide):
+        there = all_ref.at[pl.ds(0, rows), pl.ds(0, wide * columns)]
+        return remote(there, there, semaphore, hop_recv.at[other, 0], {"rep": 1 - rep})
+
+    def swapped(other):
+        there = weights_ref.at[pl.ds(pl.multiple_of(other * depth + (1 - part) * half, half), half), :]
+        return remote(there, there, part_send.at[other], part_recv.at[other], {"parts": 1 - part})
+
+    def spread_out(other):
+        there = weights_ref.at[pl.ds(pl.multiple_of(other * depth + part * half, half), half), :]
+        return remote(there, there, layer_send.at[other], layer_recv.at[other, 0], {"seq": other})
 
     def weight_block(block, m, part_of):
         top = pl.multiple_of(block * depth + part_of * half, half)
@@ -254,19 +267,15 @@
             pl.ds(pl.multiple_of(target * width, width), width),
         ]
         return remote(source, weight_block(seq, m, part),
-                      layer_send.at[target, m], layer_recv.at[seq, m], {"seq": target})
+                      layer_send.at[target], layer_recv.at[seq, m], {"seq": target})
 
     def spread_arrival(block, m):
         here = weight_block(block, m, part)
-        return remote(here, here, layer_send.at[block, m], layer_recv.at[block, m], {"seq": block})
+        return remote(here, here, layer_send.at[block], layer_recv.at[block, m], {"seq": block})
 
     def swap(block, m):
         here = weight_block(block, m, part)
-        return remote(here, here, part_send.at[block, m], part_recv.at[block, m], {"parts": 1 - part})
-
-    def swap_arrival(block, m):
-        there = weight_block(block, m, 1 - part)
-        return remote(there, there, part_send.at[block, m], part_recv.at[block, m], {"parts": 1 - part})
+        return remote(here, here, part_send.at[block], part_recv.at[block], {"parts": 1 - part})
 
     def result_rows(p):
         return pl.ds(pl.multiple_of(p * piece, piece), piece)
@@ -279,15 +288,15 @@
 
     def give(block, p):
         return remote(gated_rows(block, p), out_ref.at[result_rows(p), result_columns(seq)],
-                      out_send.at[block, p], out_recv.at[seq, p], {"seq": block})
-
-    def take(source, p):
-        here = out_ref.at[result_rows(p), result_columns(source)]
-        return remote(here, here, out_send.at[source, p], out_recv.at[source, p], {"seq": source})
+                      out_send.at[block], out_recv.at[seq], {"seq": block})
+
+    def take(source):
+        here = out_ref.at[:, result_columns(source)]
+        return remote(here, here, out_send.at[source], out_recv.at[source], {"seq": source})
 
     def keep(p):
         return pltpu.make_async_copy(
-            gated_rows(seq, p), out_ref.at[result_rows(p), result_columns(seq)], own_sem.at[p]
+            gated_rows(seq, p), out_ref.at[result_rows(p), result_columns(seq)], own_sem.at[0]
         )
 
     def inside(other):
@@ -363,6 +372,8 @@
             swap(other, m).start()
 
     toward = jnp.where(2 * seq < count, -1, 1)
+    side_lag = jnp.where(is_end, SIDE_LAG[0], SIDE_LAG[1])
+    lag = jnp.where(is_end, LAG[0], LAG[1])
     first_block = by_plane(orders, 0)
 
     @pl.when(is_end)
@@ -397,18 +408,28 @@
         def _():
             send_own(1)
 
-    for p in range(PIECES - SIDE_LAG):
-        pass_side(first_block, p)
+    for p in range(PIECES - SIDE_LAG[0]):
+        @pl.when(p < PIECES - side_lag)
+        def _():
+            pass_side(first_block, p)
+
     for fill in fills:
         fill.wait()
 
     scale_ref[...] = jnp.sqrt(one_less_exp(2.0 * rate_ref[...]))
     lane_groups = width // LANES
     chunk = piece // CHUNKS
+    step_ref[...] = jnp.exp(-rate_ref[...] * chunk)
+    for group in range(lane_groups):
+        lanes = pl.ds(group * LANES, LANES)
+        decay = jnp.exp(-rate_ref[:, lanes])
+        weight = residue_ref[:, lanes] * scale_ref[:, lanes]
+        for m in range(modes):
+            decay_ref[group, m] = jnp.broadcast_to(decay[m : m + 1, :], (CHUNKS, LANES))
+            weight_ref[group, m] = jnp.broadcast_to(weight[m : m + 1, :], (CHUNKS, LANES))
 
     def project(block, p):
-        for which in range(2):
-            core_arrival(block, which, p).wait_recv()
+        core_arrivals(block, p).wait_recv()
         top = pl.ds(pl.multiple_of(block * rows + p * piece, piece), piece)
         found = jnp.dot(all_ref[top, :], weights_ref[...], preferred_element_type=jnp.float32)
         found = found.astype(jnp.bfloat16)
@@ -425,31 +446,25 @@
         top = pl.multiple_of(g * piece, piece)
         for group in range(lane_groups):
             lanes = pl.ds(group * LANES, LANES)
-            rates = rate_ref[:, lanes]
             residues = residue_ref[:, lanes]
             scale = scale_ref[:, lanes]
-            decay = jnp.exp(-rates)
-            weight = residues * scale
-            chunk_decay = jnp.exp(-rates * chunk)
-
-            def rows_of(array):
-                return [jnp.broadcast_to(array[m : m + 1, :], (CHUNKS, LANES)) for m in range(modes)]
-
-            decays = rows_of(decay)
-            weights = rows_of(weight)
+            chunk_decay = step_ref[:, lanes]
+            decays = [decay_ref[group, m] for m in range(modes)]
+            weights = [weight_ref[group, m] for m in range(modes)]
 
             def sums(step, states):
                 here = signal[group, pl.ds(top + step, CHUNKS, stride=chunk), :]
                 return tuple(d * s + here for d, s in zip(decays, states))
 
             zero = jnp.zeros((CHUNKS, LANES), jnp.float32)
-            finals = lax.fori_loop(0, chunk, sums, (zero,) * modes, unroll=4)
+            finals = lax.fori_loop(0, chunk, sums, (zero,) * modes, unroll=UNROLL)
             for m in range(modes):
-                ends[m] = finals[m]
+                ends[pl.ds(m, CHUNKS, stride=modes), :] = finals[m]
             state = carried_ref[:, lanes]
             for c in range(CHUNKS):
-                entering[:, c, :] = residues * state
-                state = chunk_decay * state + scale * ends[:, c, :]
+                at = pl.ds(c * modes, modes)
+                entering[at, :] = residues * state
+                state = chunk_decay * state + scale * ends[at, :]
             carried_ref[:, lanes] = state
 
             def outputs(step, states):
@@ -463,8 +478,8 @@
                 conv[group, pl.ds(step, CHUNKS, stride=chunk), :] = terms[0]
                 return states
 
-            starts = tuple(entering[m] for m in range(modes))
-            lax.fori_loop(0, chunk, outputs, starts, unroll=4)
+            starts = tuple(entering[pl.ds(m, CHUNKS, stride=modes), :] for m in range(modes))
+            lax.fori_loop(0, chunk, outputs, starts, unroll=UNROLL)
             rounded = conv[group].astype(jnp.bfloat16).astype(jnp.float32)
             gated_ref[pl.ds(top, piece), lanes] = (
                 query_rows[pl.ds(top, piece), lanes].astype(jnp.float32) * rounded
@@ -517,14 +532,22 @@
                 for other in (seq - distance, seq + distance):
                     @pl.when(inside(other))
                     def _():
-                        for m in range(3):
-                            swap_arrival(other, m).wait_recv()
+                        swapped(other).wait_recv()
+
+        def next_side():
+            pass_side(block_of(k - side_lag), lax.rem(k - side_lag, PIECES))
+
+        first = is_end & (k > last)
+
+        @pl.when(first & (k < last + side_lag))
+        def _():
+            next_side()
 
         def one(which, _):
             early = which < 2
-            n = jnp.where(early, k - PIECES, k - LAG)
-            block = jnp.where(which == 0, seq, jnp.where(which == 1, first_block, block_of(k - LAG)))
-            known = (early & (n < PIECES)) | (jnp.logical_not(early) & (n >= PIECES))
+            n = jnp.where(early, k - PIECES, k - lag)
+            block = jnp.where(which == 0, seq, jnp.where(which == 1, first_block, block_of(k - lag)))
+            known = (early & (n < PIECES)) | (jnp.logical_not(early) & (n >= PIECES) & (n < last))
 
             @pl.when(known)
             def _():
@@ -536,31 +559,29 @@
         done, reach = by_plane(ready, k - PIECES), by_plane(ready, k - PIECES + 1)
         lax.fori_loop(done, reach, scan_and_send, k)
 
-        @pl.when(k >= last - 2)
+        @pl.when((k >= last - 2) & (k <= last))
         def _():
             lax.fori_loop(0, done, send_held, k)
 
-        @pl.when(k < last + SIDE_LAG)
-        def _():
-            pass_side(block_of(k - SIDE_LAG), lax.rem(k - SIDE_LAG, PIECES))
+        @pl.when(jnp.logical_not(first) & (k < last + side_lag))
+        def _():
+            next_side()
 
         return 0
 
-    lax.fori_loop(PIECES, last + LAG, slot, 0)
+    lax.fori_loop(PIECES, last + LAG[1], slot, 0)
     state_ref[...] = carried_ref[...]
 
-    for p in range(PIECES):
-        @pl.when(seq > 0)
-        def _():
-            hop(seq, p, -1, own_piece(p)).wait_send()
-
-        @pl.when(seq + 1 < count)
-        def _():
-            hop(seq, p, 1, own_piece(p)).wait_send()
-
-        side(seq, p, own_piece(p)).wait_send()
-        core(seq, 0, p, own_piece(p)).wait_send()
-        core(seq, 1, p).wait_send()
+    @pl.when(seq > 0)
+    def _():
+        sent(hop_send.at[seq, 1], seq, 1).wait_send()
+
+    @pl.when(seq + 1 < count)
+    def _():
+        sent(hop_send.at[seq, 0], seq, 1).wait_send()
+
+    sent(side_send.at[seq], seq, 1).wait_send()
+    sent(core_send.at[seq], seq, 2).wait_send()
     others = [
         (other, way)
         for distance in range(1, count)
@@ -569,29 +590,24 @@
     for other, way in others:
         @pl.when(inside(other))
         def _():
-            for m in range(3):
-                spread(other, m).wait_send()
-                swap(other, m).wait_send()
-            for p in range(PIECES):
-                @pl.when(inside(seq + way))
-                def _():
-                    hop(other, p, way).wait_send()
-
-                side(other, p).wait_send()
-                for which in range(2):
-                    core(other, which, p).wait_send()
-    for p in range(PIECES):
-        keep(p).wait()
+            @pl.when(inside(seq + way))
+            def _():
+                sent(hop_send.at[other, (1 - way) // 2], other, 1).wait_send()
+
+            sent(side_send.at[other], other, 1).wait_send()
+            sent(core_send.at[other], other, 2).wait_send()
+            spread_out(other).wait_send()
+            swapped(other).wait_send()
+    kept = out_ref.at[:, result_columns(seq)]
+    pltpu.make_async_copy(kept, kept, own_sem.at[0]).wait()
     for other, way in others:
         @pl.when(inside(other))
         def _():
-            for p in range(PIECES):
-                give(other, p).wait_send()
+            take(other).wait_send()
     for other, way in others:
         @pl.when(inside(other))
         def _():
-            for p in range(PIECES):
-                take(other, p).wait_recv()
+            take(other).wait_recv()
 
 
 def whole_layer(tokens, w_query, w_key, w_value, rate, residue, carried, count):
@@ -619,17 +635,20 @@
             pltpu.VMEM((width // LANES, length, LANES), jnp.float32),
             pltpu.VMEM((width // LANES, rows // PIECES, LANES), jnp.float32),
             pltpu.VMEM((length, width), jnp.bfloat16),
-            pltpu.VMEM((modes, CHUNKS, LANES), jnp.float32),
-            pltpu.VMEM((modes, CHUNKS, LANES), jnp.float32),
+            pltpu.VMEM((CHUNKS * modes, LANES), jnp.float32),
+            pltpu.VMEM((CHUNKS * modes, LANES), jnp.float32),
         ] + [table] * 4 + [
+            pltpu.VMEM((width // LANES, modes, CHUNKS, LANES), jnp.float32),
+            pltpu.VMEM((width // LANES, modes, CHUNKS, LANES), jnp.float32),
+            table,
             dma((7,)),
-            dma((count, PIECES, 2)), dma((count, PIECES)),
-            dma((count, PIECES)), dma((count, PIECES)),
-            dma((count, 2, PIECES)), dma((count, 2, PIECES)),
-            dma((count, 3)), dma((count, 3)),
-            dma((count, 3)), dma((count, 3)),
-            dma((count, PIECES)), dma((count, PIECES)),
-            dma((PIECES,)),
+            dma((count, 2)), dma((count, PIECES)),
+            dma((count,)), dma((count, PIECES)),
+            dma((count,)), dma((count, PIECES)),
+            dma((count,)), dma((count,)),
+            dma((count,)), dma((count, 3)),
+            dma((count,)), dma((count,)),
+            dma((1,)),
         ],
         compiler_params=pltpu.CompilerParams(
             collective_id=0, has_side_effects=True, vmem_limit_bytes=40 * 2**20

time: 150 us -> 148 us (0.987)
  no operation moved by 1% of the time
where the time goes in v4:
time: 148 us
  Pallas kernels  145 us (98%)
  local copies, waits for them, and re-layouts  1.58 us (1%)
    pallas_call x1, Pallas kernels, whole_layer(): pl.pallas_call(functools.partial(layer_kernel, count), out_shape=(jax.Sha...  145 us

profile of v4, /device:TPU:25, one launch (start us, length us, event | category | flops | bytes accessed | tf_op | source)
XLA Modules:
  0.0 147.5 jit_solution(14279637630499108705)
XLA Ops:
  0.6 145.3 %shard_map.86 = (bf16[512,1024]{1,0:T(8,128)(2,1)S(1)}, f32[16,256]{1,0:T(8,128)S(1)}) custom-call(bf16[512,1024]{1,0:T(8,128)(2,1)} %tokens_ref.1, bf16[1024,1024]{1,0:T(8,128)(2,1)} %query_ref.1, bf16[1024,1024]{1,0:T(8,128)(2,1)} %key_ref.1, bf16[1024,1024]{1,0:T(8,128)(2,1)} %value_ref.1, f32[16,256]{1,0:T(8,128)} %bitcast.5, f32[16,256]{1,0:T(8,128)} %bitcast.6, ...), custom_call_target="tpu_custom_call" | custom-call | tf_op jit(solution)/shard_map/pallas_call | solution.py:623
  145.9 1.0 copy.11
  146.9 0.6 copy.12

commit v5 on v4

--- a/solution.py
+++ b/solution.py
@@ -108,9 +108,10 @@
 
 
 PIECES = 4
-SIDE_LAG = (1, 2)
-LAG = (2, 3)
-CAP = 2
+SIDE_LAG = (1, 1)
+LAG = (2, 2)
+SHIFT = 1
+CAP = 3
 UNROLL = 8
 
 
@@ -136,7 +137,7 @@
     last = (count - 1) * PIECES
     return (
         (0, 0, last - 2, 0),
-        (last - 1, 0, 0, last - 1),
+        (last - 1, 0, last + 1, last - 1),
         (last, 0, 0, last - 1),
         (last - 1, 0, 0, 0),
     )
@@ -149,7 +150,7 @@
     for z, order in enumerate(orders):
         when = {}
         for p in range(PIECES):
-            when[z, p] = when[order[0], p] = PIECES + p
+            when[z, p] = when[order[0], p] = PIECES + p + (0 if z in (0, count - 1) else SHIFT)
             for n in range(1, count - 1):
                 when[order[n], p] = n * PIECES + p + LAG[0 if z in (0, count - 1) else 1]
         row = [0]
@@ -335,8 +336,14 @@
         for p in range(PIECES):
             hop(seq, p, way, own_piece(p)).start()
 
-    for way in (1, -1):
-        @pl.when(inside(seq + way))
+    for way, at_end in ((1, is_first), (-1, is_last)):
+        @pl.when(at_end)
+        def _():
+            send_weights(way, (1,))
+            send_own(way)
+            send_weights(way, range(count - 1, 1, -1))
+
+        @pl.when(jnp.logical_not(at_end) & inside(seq + way))
         def _():
             send_weights(way, range(count - 1, 0, -1))
             if way == 1:
@@ -374,31 +381,35 @@
     toward = jnp.where(2 * seq < count, -1, 1)
     side_lag = jnp.where(is_end, SIDE_LAG[0], SIDE_LAG[1])
     lag = jnp.where(is_end, LAG[0], LAG[1])
+    shift = jnp.where(is_end, 0, SHIFT)
     first_block = by_plane(orders, 0)
+
+    far, between = count - 1, range(count - 2, 1, -1)
 
     @pl.when(is_end)
     def _():
         for m in range(3):
             pass_side(seq, m)
-            pass_weights(seq - toward * (count - 1), m)
+            for distance in between:
+                pass_weights(seq - toward * distance, m)
         for p in range(3, PIECES):
             pass_side(seq, p)
-        for distance in range(1, count - 1):
+        for m in range(3):
+            pass_weights(seq - toward, m)
+        relay(first_block, 0)
+        if far > 1:
             for m in range(3):
-                pass_weights(seq - toward * distance, m)
-        for p in range(PIECES):
+                pass_weights(seq - toward * far, m)
+        for p in range(1, PIECES):
             relay(first_block, p)
 
     @pl.when(jnp.logical_not(is_end))
     def _():
-        for p in range(PIECES):
+        for m in range(3):
+            pass_weights(seq + toward, m)
+            pass_side(seq, m)
+        for p in range(3, PIECES):
             pass_side(seq, p)
-        for distance in range(count - 2, 1, -1):
-            for m in range(3):
-                pass_weights(seq - toward * distance, m)
-        for distance in range(count - 2, 0, -1):
-            for m in range(3):
-                pass_weights(seq + toward * distance, m)
         for p in range(PIECES):
             relay(first_block, p)
             if p < 3:
@@ -408,8 +419,17 @@
         def _():
             send_own(1)
 
+        for p in range(PIECES - SIDE_LAG[1]):
+            pass_side(first_block, p)
+        for m in range(3):
+            if m == 2:
+                relay(by_plane(orders, 1), 0)
+            for distance in between:
+                pass_weights(seq - toward * distance, m)
+                pass_weights(seq + toward * distance, m)
+
     for p in range(PIECES - SIDE_LAG[0]):
-        @pl.when(p < PIECES - side_lag)
+        @pl.when(is_end)
         def _():
             pass_side(first_block, p)
 
@@ -522,11 +542,11 @@
         return by_plane(orders, k // PIECES)
 
     def slot(k, _):
-        @pl.when(k < last)
+        @pl.when((k < last) & (is_end | (k > PIECES)))
         def _():
             relay(block_of(k), lax.rem(k, PIECES))
 
-        @pl.when(k == PIECES)
+        @pl.when(k == PIECES + shift)
         def _():
             for distance in range(1, count):
                 for other in (seq - distance, seq + distance):
@@ -545,9 +565,9 @@
 
         def one(which, _):
             early = which < 2
-            n = jnp.where(early, k - PIECES, k - lag)
+            n = jnp.where(early, k - PIECES - shift, k - lag)
             block = jnp.where(which == 0, seq, jnp.where(which == 1, first_block, block_of(k - lag)))
-            known = (early & (n < PIECES)) | (jnp.logical_not(early) & (n >= PIECES) & (n < last))
+            known = (early & (n >= 0) & (n < PIECES)) | (jnp.logical_not(early) & (n >= PIECES) & (n < last))
 
             @pl.when(known)
             def _():
@@ -559,7 +579,7 @@
         done, reach = by_plane(ready, k - PIECES), by_plane(ready, k - PIECES + 1)
         lax.fori_loop(done, reach, scan_and_send, k)
 
-        @pl.when((k >= last - 2) & (k <= last))
+        @pl.when((k >= last - 2) & (k <= last + 1))
         def _():
             lax.fori_loop(0, done, send_held, k)
 

time: 148 us -> 146 us (0.986)
  Pallas kernels: 145 us -> 143 us
    pallas_call x1, Pallas kernels: 145 us -> 143 us  [whole_layer(): pl.pallas_call(functools.partial(layer_kernel, count), out_shape=(jax.Sha...]
where the time goes in v5:
time: 146 us; the launch traced here: 145 us
  Pallas kernels  143 us (98%)
  local copies, waits for them, and re-layouts  1.58 us (1%)
    pallas_call x1, Pallas kernels, whole_layer(): pl.pallas_call(functools.partial(layer_kernel, count), out_shape=(jax.Sha...  143 us

profile of v5, /device:TPU:25, one launch (start us, length us, event | category | flops | bytes accessed | tf_op | source)
XLA Modules:
  0.0 145.2 jit_solution(2891646904900390731)
XLA Ops:
  0.6 143.0 %shard_map.86 = (bf16[512,1024]{1,0:T(8,128)(2,1)S(1)}, f32[16,256]{1,0:T(8,128)S(1)}) custom-call(bf16[512,1024]{1,0:T(8,128)(2,1)} %tokens_ref.1, bf16[1024,1024]{1,0:T(8,128)(2,1)} %query_ref.1, bf16[1024,1024]{1,0:T(8,128)(2,1)} %key_ref.1, bf16[1024,1024]{1,0:T(8,128)(2,1)} %value_ref.1, f32[16,256]{1,0:T(8,128)} %bitcast.5, f32[16,256]{1,0:T(8,128)} %bitcast.6, ...), custom_call_target="tpu_custom_call" | custom-call | tf_op jit(solution)/shard_map/pallas_call | solution.py:643
  143.7 1.0 copy.11
  144.6 0.6 copy.12

commit v6 on v5

--- a/solution.py
+++ b/solution.py
@@ -527,14 +527,20 @@
     def release(block):
         return by_plane(releases, block)
 
-    def send_held(g, k):
-        block = g // PIECES
-
-        @pl.when((block != seq) & (release(block) == k))
-        def _():
-            give(block, lax.rem(g, PIECES)).start()
-
-        return k
+    def send_held(k, done):
+        for block in range(count):
+            due = pick([row[block] for row in releases], seq)
+
+            @pl.when((seq != block) & (due == k))
+            def _():
+                def send(p, _):
+                    @pl.when(block * PIECES + p < done)
+                    def _():
+                        give(block, p).start()
+
+                    return 0
+
+                lax.fori_loop(0, PIECES, send, 0)
 
     last = (count - 1) * PIECES
 
@@ -581,7 +587,7 @@
 
         @pl.when((k >= last - 2) & (k <= last + 1))
         def _():
-            lax.fori_loop(0, done, send_held, k)
+            send_held(k, done)
 
         @pl.when(jnp.logical_not(first) & (k < last + side_lag))
         def _():
@@ -674,7 +680,38 @@
             collective_id=0, has_side_effects=True, vmem_limit_bytes=40 * 2**20
         ),
     )(*(pltpu.with_memory_space_constraint(array, pltpu.HBM) for array in operands))
-    return gated, state.T
+    return settle(gated, state)
+
+
+def settle_kernel(gated_ref, state_ref, out_ref, final_ref, sem):
+    rows = gated_ref.shape[0]
+    part = rows // PIECES
+    copies = [
+        pltpu.make_async_copy(
+            gated_ref.at[pl.ds(p * part, part), :], out_ref.at[pl.ds(p * part, part), :], sem.at[p]
+        )
+        for p in range(PIECES)
+    ] + [pltpu.make_async_copy(state_ref, final_ref, sem.at[PIECES])]
+    for copy in copies:
+        copy.start()
+    for copy in copies:
+        copy.wait()
+
+
+def settle(gated, state):
+    anywhere = pl.BlockSpec(memory_space=pl.ANY)
+    out, final = pl.pallas_call(
+        settle_kernel,
+        out_shape=(
+            jax.ShapeDtypeStruct(gated.shape, gated.dtype),
+            jax.ShapeDtypeStruct(state.shape, state.dtype),
+        ),
+        in_specs=[anywhere] * 2,
+        out_specs=(anywhere, anywhere),
+        scratch_shapes=[pltpu.SemaphoreType.DMA((PIECES + 1,))],
+        compiler_params=pltpu.CompilerParams(vmem_limit_bytes=2**20),
+    )(gated, state)
+    return out, final.T
 
 
 def per_device_channels(tokens, w_query, w_key, w_value, decay_rate, residue, carried):

time: 146 us -> 145 us (level)
  local copies, waits for them, and re-layouts: 1.58 us -> 0 us
    unnamed x2 -> x0, local copies, waits for them, and re-layouts: 1.58 us -> none
where the time goes in v6:
time: 145 us; the launch traced here: 144 us
  Pallas kernels  144 us (99%)
    pallas_call x1, Pallas kernels, whole_layer(): pl.pallas_call(functools.partial(layer_kernel, count), out_shape=(jax.Sha...  143 us

profile of v6, /device:TPU:25, one launch (start us, length us, event | category | flops | bytes accessed | tf_op | source)
XLA Modules:
  0.0 144.5 jit_solution(7901308137564128307)
XLA Ops:
  0.6 142.8 %shard_map.86 = (bf16[512,1024]{1,0:T(8,128)(2,1)S(1)}, f32[16,256]{1,0:T(8,128)S(1)}) custom-call(bf16[512,1024]{1,0:T(8,128)(2,1)} %tokens_ref.1, bf16[1024,1024]{1,0:T(8,128)(2,1)} %query_ref.1, bf16[1024,1024]{1,0:T(8,128)(2,1)} %key_ref.1, bf16[1024,1024]{1,0:T(8,128)(2,1)} %value_ref.1, f32[16,256]{1,0:T(8,128)} %bitcast.4, f32[16,256]{1,0:T(8,128)} %bitcast.5, ...), custom_call_target="tpu_custom_call" | custom-call | tf_op jit(solution)/shard_map/pallas_call | solution.py:649
  143.5 1.0 shard_map.87

commit v7 on v6

--- a/solution.py
+++ b/solution.py
@@ -110,8 +110,8 @@
 PIECES = 4
 SIDE_LAG = (1, 1)
 LAG = (2, 2)
-SHIFT = 1
-CAP = 3
+SHIFT = 0
+CAP = 2
 UNROLL = 8
 
 
@@ -138,7 +138,7 @@
     return (
         (0, 0, last - 2, 0),
         (last - 1, 0, last + 1, last - 1),
-        (last, 0, 0, last - 1),
+        (last, 0, 0, last - 2),
         (last - 1, 0, 0, 0),
     )
 
@@ -168,8 +168,8 @@
                  carried_hbm, out_ref, state_ref,
                  all_ref, weights_ref, query_rows, signal, conv, gated_ref, ends, entering,
                  rate_ref, scale_ref, residue_ref, carried_ref, decay_ref, weight_ref, step_ref,
-                 fill_sem, hop_send, hop_recv, side_send, side_recv, core_send, core_recv,
-                 part_send, part_recv, layer_send, layer_recv, out_send, out_recv, own_sem):
+                 fill_sem, hop_send, hop_recv, side_send, side_recv, core_recv,
+                 part_recv, layer_send, layer_recv, out_send, out_recv, own_sem):
     part, seq, chan, rep = (lax.axis_index(a) for a in ("parts", "seq", "chan", "rep"))
     rows, columns = tokens_ref.shape
     depth, outer = query_ref.shape
@@ -239,12 +239,12 @@
     def core(block, which, p, source=None):
         here = token_block(block, chan if which == 0 else 1 - chan, rep, p)
         return remote(here if source is None else source, here,
-                      core_send.at[block], core_recv.at[block, p], {"rep": 1 - rep})
+                      side_send.at[block], core_recv.at[block, p], {"rep": 1 - rep})
 
     def core_arrivals(block, p):
         top = pl.multiple_of(block * rows + p * piece, piece)
         there = all_ref.at[pl.ds(top, piece), pl.ds(0, 2 * columns)]
-        return remote(there, there, core_send.at[block], core_recv.at[block, p], {"rep": 1 - rep})
+        return remote(there, there, side_send.at[block], core_recv.at[block, p], {"rep": 1 - rep})
 
     def sent(semaphore, other, wide):
         there = all_ref.at[pl.ds(0, rows), pl.ds(0, wide * columns)]
@@ -252,10 +252,10 @@
 
     def swapped(other):
         there = weights_ref.at[pl.ds(pl.multiple_of(other * depth + (1 - part) * half, half), half), :]
-        return remote(there, there, part_send.at[other], part_recv.at[other], {"parts": 1 - part})
-
-    def spread_out(other):
-        there = weights_ref.at[pl.ds(pl.multiple_of(other * depth + part * half, half), half), :]
+        return remote(there, there, layer_send.at[other], part_recv.at[other], {"parts": 1 - part})
+
+    def weights_sent(other):
+        there = weights_ref.at[pl.ds(pl.multiple_of(other * depth, depth), depth), :]
         return remote(there, there, layer_send.at[other], layer_recv.at[other, 0], {"seq": other})
 
     def weight_block(block, m, part_of):
@@ -276,7 +276,7 @@
 
     def swap(block, m):
         here = weight_block(block, m, part)
-        return remote(here, here, part_send.at[block], part_recv.at[block], {"parts": 1 - part})
+        return remote(here, here, layer_send.at[block], part_recv.at[block], {"parts": 1 - part})
 
     def result_rows(p):
         return pl.ds(pl.multiple_of(p * piece, piece), piece)
@@ -319,8 +319,6 @@
     is_end = is_first | is_last
     deferred = (seq == 1) if count == 4 else (seq == count)
 
-    for fill in fills:
-        fill.start()
     pl.semaphore_wait(barrier, count - 1 + len(mates))
 
     def send_weights(way, distances):
@@ -341,7 +339,7 @@
         def _():
             send_weights(way, (1,))
             send_own(way)
-            send_weights(way, range(count - 1, 1, -1))
+            send_weights(way, range(2, count))
 
         @pl.when(jnp.logical_not(at_end) & inside(seq + way))
         def _():
@@ -356,6 +354,8 @@
     for p in range(PIECES):
         side(seq, p, own_piece(p)).start()
         core(seq, 0, p, own_piece(p)).start()
+    for fill in fills:
+        fill.start()
 
     def relay(block, p):
         way = jnp.where(block < seq, 1, -1)
@@ -396,12 +396,11 @@
             pass_side(seq, p)
         for m in range(3):
             pass_weights(seq - toward, m)
-        relay(first_block, 0)
+        for p in range(PIECES):
+            relay(first_block, p)
         if far > 1:
             for m in range(3):
                 pass_weights(seq - toward * far, m)
-        for p in range(1, PIECES):
-            relay(first_block, p)
 
     @pl.when(jnp.logical_not(is_end))
     def _():
@@ -422,8 +421,6 @@
         for p in range(PIECES - SIDE_LAG[1]):
             pass_side(first_block, p)
         for m in range(3):
-            if m == 2:
-                relay(by_plane(orders, 1), 0)
             for distance in between:
                 pass_weights(seq - toward * distance, m)
                 pass_weights(seq + toward * distance, m)
@@ -548,7 +545,7 @@
         return by_plane(orders, k // PIECES)
 
     def slot(k, _):
-        @pl.when((k < last) & (is_end | (k > PIECES)))
+        @pl.when((k < last) & (k >= PIECES))
         def _():
             relay(block_of(k), lax.rem(k, PIECES))
 
@@ -606,8 +603,7 @@
     def _():
         sent(hop_send.at[seq, 0], seq, 1).wait_send()
 
-    sent(side_send.at[seq], seq, 1).wait_send()
-    sent(core_send.at[seq], seq, 2).wait_send()
+    sent(side_send.at[seq], seq, 3).wait_send()
     others = [
         (other, way)
         for distance in range(1, count)
@@ -620,10 +616,8 @@
             def _():
                 sent(hop_send.at[other, (1 - way) // 2], other, 1).wait_send()
 
-            sent(side_send.at[other], other, 1).wait_send()
-            sent(core_send.at[other], other, 2).wait_send()
-            spread_out(other).wait_send()
-            swapped(other).wait_send()
+            sent(side_send.at[other], other, 3).wait_send()
+            weights_sent(other).wait_send()
     kept = out_ref.at[:, result_columns(seq)]
     pltpu.make_async_copy(kept, kept, own_sem.at[0]).wait()
     for other, way in others:
@@ -670,8 +664,8 @@
             dma((7,)),
             dma((count, 2)), dma((count, PIECES)),
             dma((count,)), dma((count, PIECES)),
-            dma((count,)), dma((count, PIECES)),
-            dma((count,)), dma((count,)),
+            dma((count, PIECES)),
+            dma((count,)),
             dma((count,)), dma((count, 3)),
             dma((count,)), dma((count,)),
             dma((1,)),

time: 145 us -> 145 us (level)
  no operation moved by 1% of the time
where the time goes in v7:
time: 145 us; the launch traced here: 144 us
  Pallas kernels  143 us (99%)
    pallas_call x1, Pallas kernels, whole_layer(): pl.pallas_call(functools.partial(layer_kernel, count), out_shape=(jax.Sha...  142 us

profile of v7, /device:TPU:25, one launch (start us, length us, event | category | flops | bytes accessed | tf_op | source)
XLA Modules:
  0.0 144.0 jit_solution(16489912273741450590)
XLA Ops:
  0.6 142.4 %shard_map.86 = (bf16[512,1024]{1,0:T(8,128)(2,1)S(1)}, f32[16,256]{1,0:T(8,128)S(1)}) custom-call(bf16[512,1024]{1,0:T(8,128)(2,1)} %tokens_ref.1, bf16[1024,1024]{1,0:T(8,128)(2,1)} %query_ref.1, bf16[1024,1024]{1,0:T(8,128)(2,1)} %key_ref.1, bf16[1024,1024]{1,0:T(8,128)(2,1)} %value_ref.1, f32[16,256]{1,0:T(8,128)} %bitcast.4, f32[16,256]{1,0:T(8,128)} %bitcast.5, ...), custom_call_target="tpu_custom_call" | custom-call | tf_op jit(solution)/shard_map/pallas_call | solution.py:643
  143.0 1.0 shard_map.87

commit v8 on v7

--- a/solution.py
+++ b/solution.py
@@ -138,7 +138,7 @@
     return (
         (0, 0, last - 2, 0),
         (last - 1, 0, last + 1, last - 1),
-        (last, 0, 0, last - 2),
+        (last, 0, 0, 0),
         (last - 1, 0, 0, 0),
     )
 

time: 145 us -> 145 us (level)
  no operation moved by 1% of the time
where the time goes in v8:
time: 145 us; the launch traced here: 144 us
  Pallas kernels  143 us (99%)
    pallas_call x1, Pallas kernels, whole_layer(): pl.pallas_call(functools.partial(layer_kernel, count), out_shape=(jax.Sha...  142 us

profile of v8, /device:TPU:25, one launch (start us, length us, event | category | flops | bytes accessed | tf_op | source)
XLA Modules:
  0.0 144.0 jit_solution(6707973749784321042)
XLA Ops:
  0.6 142.4 %shard_map.86 = (bf16[512,1024]{1,0:T(8,128)(2,1)S(1)}, f32[16,256]{1,0:T(8,128)S(1)}) custom-call(bf16[512,1024]{1,0:T(8,128)(2,1)} %tokens_ref.1, bf16[1024,1024]{1,0:T(8,128)(2,1)} %query_ref.1, bf16[1024,1024]{1,0:T(8,128)(2,1)} %key_ref.1, bf16[1024,1024]{1,0:T(8,128)(2,1)} %value_ref.1, f32[16,256]{1,0:T(8,128)} %bitcast.4, f32[16,256]{1,0:T(8,128)} %bitcast.5, ...), custom_call_target="tpu_custom_call" | custom-call | tf_op jit(solution)/shard_map/pallas_call | solution.py:643
  143.0 1.0 shard_map.87
